TPU v7x, 128 devices: a whole 4x4x4 slice. The times are simulated.
128 devices in a mesh: layer: 16 (over x, z), row: 2 (over y_hi), col: 4 (over y_lo, core).
Axes of the slice: x: 4, y: 4 (y_hi: 2, y_lo: 2; y = y_hi * 2 + y_lo), z: 4, core: 2. Of those that a mesh axis runs over, the one named last changes fastest.
Arguments:
- c_guess: float32 [16, 1, 64, 16, 512], P('layer', None, None, 'row', 'col'), may hold values from -6 to 6
- adjoint_guess: float32 [16, 1, 64, 16, 512], P('layer', None, None, 'row', 'col'), may hold values from -6 to 6
- weights: bfloat16 [128, 9, 64, 64], P('layer'), may hold values from -0.25 to 0.25
- biases: float32 [128, 64], P('layer'), may hold values from -2 to 2
- coarse_gain: float32 [16, 64], P('layer'), may hold values from 0 to 1
Outputs:
- c_states: float32 [16, 1, 64, 16, 512], P('layer', None, None, 'row', 'col')
- adjoint_ends: float32 [16, 1, 64, 16, 512], P('layer', None, None, 'row', 'col')
- weight_grad: float32 [128, 9, 64, 64], P('layer')
All inputs are finite; a program needn't handle non-finite values.
Results may differ from a plain program's by a relative error of at most 0.0049.
Values may be sent and summed in bfloat16 or wider, within the bound.
A program may use at most 128 MiB of HBM per device.

v0:
```python
import jax
import jax.numpy as jnp
from jax import lax
from jax.sharding import PartitionSpec as P

step_size = 0.5


def with_halo(block, sides, width):
    for axis, dim in sides:
        count = lax.axis_size(axis)
        forward = [(i, i + 1) for i in range(count - 1)]
        backward = [(target, source) for source, target in forward]
        low = lax.ppermute(
            lax.slice_in_dim(block, block.shape[dim] - width, None, axis=dim), axis, forward
        )
        high = lax.ppermute(lax.slice_in_dim(block, 0, width, axis=dim), axis, backward)
        block = jnp.concatenate([low, block, high], axis=dim)
    return block


def passed_along(value, axis, steps):
    count = lax.axis_size(axis)
    initial, last = (max(0, -steps), min(count, count - steps))
    return lax.ppermute(value, axis, [(source, source + steps) for source in range(initial, last)])


def convolve(padded, kernel):
    rows = padded.shape[2] - 2
    cols = padded.shape[3] - 2
    total = jnp.zeros((padded.shape[0], kernel.shape[1], rows, cols), jnp.float32)
    for tap_idx in range(9):
        row_off = tap_idx // 3
        col_off = tap_idx % 3
        window = padded[:, :, row_off : row_off + rows, col_off : col_off + cols]
        total = total + jnp.einsum(
            "oc,bchw->bohw", kernel[tap_idx], window, preferred_element_type=jnp.float32
        )
    return total


def convolve_back(padded, kernel):
    rows = padded.shape[2] - 2
    cols = padded.shape[3] - 2
    total = jnp.zeros((padded.shape[0], kernel.shape[2], rows, cols), jnp.float32)
    for tap_idx in range(9):
        row_off = 2 - tap_idx // 3
        col_off = 2 - tap_idx % 3
        window = padded[:, :, row_off : row_off + rows, col_off : col_off + cols]
        total = total + jnp.einsum(
            "oc,bohw->bchw", kernel[tap_idx], window, preferred_element_type=jnp.float32
        )
    return total


def kernel_grad(cotan, padded):
    rows = cotan.shape[2]
    cols = cotan.shape[3]
    taps = []
    for tap_idx in range(9):
        row_off = tap_idx // 3
        col_off = tap_idx % 3
        window = padded[:, :, row_off : row_off + rows, col_off : col_off + cols]
        taps.append(jnp.einsum("bohw,bchw->oc", cotan, window, preferred_element_type=jnp.float32))
    return step_size * jnp.stack(taps)


def local(c_guess, adjoint_guess, weights, biases, coarse_gain):
    blocks_here = weights.shape[0]
    start = c_guess[0]
    state = start
    states = []
    paddeds = []
    for block_idx in range(blocks_here):
        active = jnp.tanh(state).astype(jnp.bfloat16)
        padded = with_halo(active, (("row", 2), ("col", 3)), 1)
        states.append(state)
        paddeds.append(padded)
        state = state + step_size * (
            convolve(padded, weights[block_idx]) + biases[block_idx][None, :, None, None]
        )
    final_boundary = adjoint_guess[0]
    cotan = final_boundary
    grads = [None] * blocks_here
    for block_idx in reversed(range(blocks_here)):
        cot_bf = cotan.astype(jnp.bfloat16)
        grads[block_idx] = kernel_grad(cot_bf, paddeds[block_idx])
        padded_cot = with_halo(cot_bf, (("row", 2), ("col", 3)), 1)
        back = convolve_back(padded_cot, weights[block_idx])
        slope = jnp.tanh(states[block_idx])
        cotan = cotan + step_size * (1.0 - slope * slope) * back
    weight_grad = lax.psum(jnp.stack(grads), ("row", "col"))
    gain_vec = coarse_gain[0]
    gain = gain_vec[None, :, None, None]
    forward_rest = state - gain * start
    backward_rest = cotan - gain * final_boundary
    index = lax.axis_index("layer")
    count = lax.axis_size("layer")
    is_first = index == 0
    is_last = index == count - 1

    def forward_step(step_idx, current):
        received = passed_along(gain * current + forward_rest, "layer", 1)
        return jnp.where(is_first, start, received)

    def backward_step(step_idx, current):
        received = passed_along(gain * current + backward_rest, "layer", -1)
        return jnp.where(is_last, final_boundary, received)

    coarse_state = lax.fori_loop(0, count - 1, forward_step, start)
    rough_costate = lax.fori_loop(0, count - 1, backward_step, final_boundary)
    return (coarse_state[None], rough_costate[None], weight_grad)


def solution(mesh):
    in_specs = (
        P("layer", None, None, "row", "col"),
        P("layer", None, None, "row", "col"),
        P("layer", None, None, None),
        P("layer", None),
        P("layer", None),
    )
    out_specs = (
        P("layer", None, None, "row", "col"),
        P("layer", None, None, "row", "col"),
        P("layer", None, None, None),
    )
    return jax.shard_map(local, mesh=mesh, in_specs=in_specs, out_specs=out_specs, check_vma=False)
```

profile of v0, /device:TPU:104, one launch (start us, length us, event | category | flops | bytes accessed | tf_op | source)
XLA Modules:
  0.0 665.5 jit_solution(8763688313370171344)
XLA Ops:
  322.2 162.2 %while.20 = (s32[]{:T(128)}, f32[1,64,8,128]{3,2,1,0:T(8,128)S(1)}, pred[]{:T(512)}, f32[1,64,1,1]{1,3,2,0:T(1,128)S(1)}, f32[1,64,8,128]{3,2,1,0:T(8,128)S(1)}, /*index=5*/f32[1,64,8,128]{3,2,1,0:T(8,128)S(1)}, s32[]{:T(128)}) while((s32[]{:T(128)}, f32[1,64,8,128]{3,2,1,0:T(8,128)S(1)}, pred[]{:T(512)}, f32[1,64,1,1]{1,3,2,0:T(1,128)S(1)}, ...), condition=%wide.region_1.2_spmd, body=%wide.region_0.0_spmd.sunk | while | flops 196610 | bytes 2621814 | solution.py:110
  360.5 6.5 collective-permute-start
  372.6 6.5 collective-permute-start
  379.2 6.6 collective-permute-done
  385.9 6.5 collective-permute-start
  398.4 6.5 collective-permute-start
  410.1 6.5 collective-permute-start
  420.9 6.5 collective-permute-start
  485.1 170.1 %while.21 = (s32[]{:T(128)}, f32[1,64,8,128]{3,2,1,0:T(8,128)S(1)}, pred[]{:T(512)}, f32[1,64,1,1]{1,3,2,0:T(1,128)S(1)}, f32[1,64,8,128]{3,2,1,0:T(8,128)S(1)}, /*index=5*/f32[1,64,8,128]{3,2,1,0:T(8,128)S(1)}, s32[]{:T(128)}) while((s32[]{:T(128)}, f32[1,64,8,128]{3,2,1,0:T(8,128)S(1)}, pred[]{:T(512)}, f32[1,64,1,1]{1,3,2,0:T(1,128)S(1)}, ...), condition=%wide.region_3.4_spmd, body=%wide.region_2.3_spmd.sunk | while | flops 196610 | bytes 2621814 | solution.py:111
  487.2 11.1 %collective-permute-done.1 = f32[1,64,8,128]{3,2,1,0:T(8,128)S(1)} collective-permute-done((f32[1,64,8,128]{3,2,1,0:T(8,128)S(1)}, f32[1,64,8,128]{3,2,1,0:T(8,128)S(1)}, u32[]{:S(2)}, u32[]{:S(2)}) %collective-permute-start.1) | collective-permute-done | bytes 262176 | tf_op jit(solution)/shard_map/while/body/eval_jaxpr/ppermute | solution.py:25
  500.3 9.8 %collective-permute-done.1 = f32[1,64,8,128]{3,2,1,0:T(8,128)S(1)} collective-permute-done((f32[1,64,8,128]{3,2,1,0:T(8,128)S(1)}, f32[1,64,8,128]{3,2,1,0:T(8,128)S(1)}, u32[]{:S(2)}, u32[]{:S(2)}) %collective-permute-start.1) | collective-permute-done | bytes 262176 | tf_op jit(solution)/shard_map/while/body/eval_jaxpr/ppermute | solution.py:25
  512.2 8.9 %collective-permute-done.1 = f32[1,64,8,128]{3,2,1,0:T(8,128)S(1)} collective-permute-done((f32[1,64,8,128]{3,2,1,0:T(8,128)S(1)}, f32[1,64,8,128]{3,2,1,0:T(8,128)S(1)}, u32[]{:S(2)}, u32[]{:S(2)}) %collective-permute-start.1) | collective-permute-done | bytes 262176 | tf_op jit(solution)/shard_map/while/body/eval_jaxpr/ppermute | solution.py:25
  523.2 8.4 %collective-permute-done.1 = f32[1,64,8,128]{3,2,1,0:T(8,128)S(1)} collective-permute-done((f32[1,64,8,128]{3,2,1,0:T(8,128)S(1)}, f32[1,64,8,128]{3,2,1,0:T(8,128)S(1)}, u32[]{:S(2)}, u32[]{:S(2)}) %collective-permute-start.1) | collective-permute-done | bytes 262176 | tf_op jit(solution)/shard_map/while/body/eval_jaxpr/ppermute | solution.py:25
  533.8 8.4 %collective-permute-done.1 = f32[1,64,8,128]{3,2,1,0:T(8,128)S(1)} collective-permute-done((f32[1,64,8,128]{3,2,1,0:T(8,128)S(1)}, f32[1,64,8,128]{3,2,1,0:T(8,128)S(1)}, u32[]{:S(2)}, u32[]{:S(2)}) %collective-permute-start.1) | collective-permute-done | bytes 262176 | tf_op jit(solution)/shard_map/while/body/eval_jaxpr/ppermute | solution.py:25
  544.3 8.4 %collective-permute-done.1 = f32[1,64,8,128]{3,2,1,0:T(8,128)S(1)} collective-permute-done((f32[1,64,8,128]{3,2,1,0:T(8,128)S(1)}, f32[1,64,8,128]{3,2,1,0:T(8,128)S(1)}, u32[]{:S(2)}, u32[]{:S(2)}) %collective-permute-start.1) | collective-permute-done | bytes 262176 | tf_op jit(solution)/shard_map/while/body/eval_jaxpr/ppermute | solution.py:25
  554.9 8.5 %collective-permute-done.1 = f32[1,64,8,128]{3,2,1,0:T(8,128)S(1)} collective-permute-done((f32[1,64,8,128]{3,2,1,0:T(8,128)S(1)}, f32[1,64,8,128]{3,2,1,0:T(8,128)S(1)}, u32[]{:S(2)}, u32[]{:S(2)}) %collective-permute-start.1) | collective-permute-done | bytes 262176 | tf_op jit(solution)/shard_map/while/body/eval_jaxpr/ppermute | solution.py:25
  565.5 9.6 %collective-permute-done.1 = f32[1,64,8,128]{3,2,1,0:T(8,128)S(1)} collective-permute-done((f32[1,64,8,128]{3,2,1,0:T(8,128)S(1)}, f32[1,64,8,128]{3,2,1,0:T(8,128)S(1)}, u32[]{:S(2)}, u32[]{:S(2)}) %collective-permute-start.1) | collective-permute-done | bytes 262176 | tf_op jit(solution)/shard_map/while/body/eval_jaxpr/ppermute | solution.py:25
  577.3 10.8 %collective-permute-done.1 = f32[1,64,8,128]{3,2,1,0:T(8,128)S(1)} collective-permute-done((f32[1,64,8,128]{3,2,1,0:T(8,128)S(1)}, f32[1,64,8,128]{3,2,1,0:T(8,128)S(1)}, u32[]{:S(2)}, u32[]{:S(2)}) %collective-permute-start.1) | collective-permute-done | bytes 262176 | tf_op jit(solution)/shard_map/while/body/eval_jaxpr/ppermute | solution.py:25
  590.2 10.5 %collective-permute-done.1 = f32[1,64,8,128]{3,2,1,0:T(8,128)S(1)} collective-permute-done((f32[1,64,8,128]{3,2,1,0:T(8,128)S(1)}, f32[1,64,8,128]{3,2,1,0:T(8,128)S(1)}, u32[]{:S(2)}, u32[]{:S(2)}) %collective-permute-start.1) | collective-permute-done | bytes 262176 | tf_op jit(solution)/shard_map/while/body/eval_jaxpr/ppermute | solution.py:25
  602.9 9.7 %collective-permute-done.1 = f32[1,64,8,128]{3,2,1,0:T(8,128)S(1)} collective-permute-done((f32[1,64,8,128]{3,2,1,0:T(8,128)S(1)}, f32[1,64,8,128]{3,2,1,0:T(8,128)S(1)}, u32[]{:S(2)}, u32[]{:S(2)}) %collective-permute-start.1) | collective-permute-done | bytes 262176 | tf_op jit(solution)/shard_map/while/body/eval_jaxpr/ppermute | solution.py:25
  614.7 8.8 %collective-permute-done.1 = f32[1,64,8,128]{3,2,1,0:T(8,128)S(1)} collective-permute-done((f32[1,64,8,128]{3,2,1,0:T(8,128)S(1)}, f32[1,64,8,128]{3,2,1,0:T(8,128)S(1)}, u32[]{:S(2)}, u32[]{:S(2)}) %collective-permute-start.1) | collective-permute-done | bytes 262176 | tf_op jit(solution)/shard_map/while/body/eval_jaxpr/ppermute | solution.py:25
  625.6 8.4 %collective-permute-done.1 = f32[1,64,8,128]{3,2,1,0:T(8,128)S(1)} collective-permute-done((f32[1,64,8,128]{3,2,1,0:T(8,128)S(1)}, f32[1,64,8,128]{3,2,1,0:T(8,128)S(1)}, u32[]{:S(2)}, u32[]{:S(2)}) %collective-permute-start.1) | collective-permute-done | bytes 262176 | tf_op jit(solution)/shard_map/while/body/eval_jaxpr/ppermute | solution.py:25
  636.1 8.4 %collective-permute-done.1 = f32[1,64,8,128]{3,2,1,0:T(8,128)S(1)} collective-permute-done((f32[1,64,8,128]{3,2,1,0:T(8,128)S(1)}, f32[1,64,8,128]{3,2,1,0:T(8,128)S(1)}, u32[]{:S(2)}, u32[]{:S(2)}) %collective-permute-start.1) | collective-permute-done | bytes 262176 | tf_op jit(solution)/shard_map/while/body/eval_jaxpr/ppermute | solution.py:25
  646.7 8.4 %collective-permute-done.1 = f32[1,64,8,128]{3,2,1,0:T(8,128)S(1)} collective-permute-done((f32[1,64,8,128]{3,2,1,0:T(8,128)S(1)}, f32[1,64,8,128]{3,2,1,0:T(8,128)S(1)}, u32[]{:S(2)}, u32[]{:S(2)}) %collective-permute-start.1) | collective-permute-done | bytes 262176 | tf_op jit(solution)/shard_map/while/body/eval_jaxpr/ppermute | solution.py:25
  (575 shorter events, 463.3 us)
Async XLA Ops:
  7.2 648.0 %all-reduce.2.cloned.1.call-start = ((), (), s32[]{:S(2)}) async-start(), calls=%async_computation | async-start | bytes 4718592 | tf_op jit(solution)/shard_map/psum | solution.py:92
  8.3 16.1 %collective-permute-start.2 = (bf16[1,64,1,128]{3,1,2,0:T(8,128)(2,1)S(1)}, bf16[1,64,1,128]{3,1,2,0:T(8,128)(2,1)S(1)}, u32[]{:S(2)}, u32[]{:S(2)}) collective-permute-start(bf16[1,64,1,128]{3,1,2,0:T(8,128)(2,1)S(1)} %get-tuple-element.199), channel_id=1, source_target_pairs={{0,4},{1,5},{2,6},{3,7},{8,12},{9,13},{10,14},{11,15},{16,20},{17,... | collective-permute-start | bytes 49160 | tf_op jit(solution)/shard_map/ppermute | solution.py:14
  12.5 11.9 %collective-permute-start.3 = (bf16[1,64,1,128]{3,1,2,0:T(8,128)(2,1)S(1)}, bf16[1,64,1,128]{3,1,2,0:T(8,128)(2,1)S(1)}, u32[]{:S(2)}, u32[]{:S(2)}) collective-permute-start(bf16[1,64,1,128]{3,1,2,0:T(8,128)(2,1)S(1)} %get-tuple-element.200), channel_id=1, source_target_pairs={{4,0},{5,1},{6,2},{7,3},{12,8},{13,9},{14,10},{15,11},{20,16},{21,... | collective-permute-start | bytes 49160 | tf_op jit(solution)/shard_map/ppermute | solution.py:17
  14.8 15.4 %collective-permute-start.34 = (bf16[1,64,1,128]{3,1,2,0:T(8,128)(2,1)S(1)}, bf16[1,64,1,128]{3,1,2,0:T(8,128)(2,1)S(1)}, u32[]{:S(2)}, u32[]{:S(2)}) collective-permute-start(bf16[1,64,1,128]{3,1,2,0:T(8,128)(2,1)S(1)} %get-tuple-element.183), channel_id=1, source_target_pairs={{0,4},{1,5},{2,6},{3,7},{8,12},{9,13},{10,14},{11,15},{16,20},{17,... | collective-permute-start | bytes 49160 | tf_op jit(solution)/shard_map/ppermute | solution.py:14
  30.5 14.1 %collective-permute-start.36 = (bf16[1,64,10,1]{3,1,2,0:T(8,128)(2,1)S(1)}, bf16[1,64,10,1]{3,1,2,0:T(8,128)(2,1)S(1)}, u32[]{:S(2)}, u32[]{:S(2)}) collective-permute-start(bf16[1,64,10,1]{3,1,2,0:T(8,128)(2,1)S(1)} %get-tuple-element.135), channel_id=1, source_target_pairs={{1,0},{2,1},{3,2},{5,4},{6,5},{7,6},{9,8},{10,9},{11,10},{13,12},{... | collective-permute-start | bytes 3848 | tf_op jit(solution)/shard_map/ppermute | solution.py:17
  32.4 12.2 %collective-permute-start.37 = (bf16[1,64,10,1]{3,1,2,0:T(8,128)(2,1)S(1)}, bf16[1,64,10,1]{3,1,2,0:T(8,128)(2,1)S(1)}, u32[]{:S(2)}, u32[]{:S(2)}) collective-permute-start(bf16[1,64,10,1]{3,1,2,0:T(8,128)(2,1)S(1)} %get-tuple-element.136), channel_id=1, source_target_pairs={{0,1},{1,2},{2,3},{4,5},{5,6},{6,7},{8,9},{9,10},{10,11},{12,13},{... | collective-permute-start | bytes 3848 | tf_op jit(solution)/shard_map/ppermute | solution.py:14
  156.9 12.4 %collective-permute-start.30 = (bf16[1,64,1,128]{3,1,2,0:T(8,128)(2,1)S(1)}, bf16[1,64,1,128]{3,1,2,0:T(8,128)(2,1)S(1)}, u32[]{:S(2)}, u32[]{:S(2)}) collective-permute-start(bf16[1,64,1,128]{3,1,2,0:T(8,128)(2,1)S(1)} %get-tuple-element.185), channel_id=1, source_target_pairs={{0,4},{1,5},{2,6},{3,7},{8,12},{9,13},{10,14},{11,15},{16,20},{17,... | collective-permute-start | bytes 49160 | tf_op jit(solution)/shard_map/ppermute | solution.py:14
  162.0 13.1 %collective-permute-start.39 = (bf16[1,64,1,128]{3,1,2,0:T(8,128)(2,1)S(1)}, bf16[1,64,1,128]{3,1,2,0:T(8,128)(2,1)S(1)}, u32[]{:S(2)}, u32[]{:S(2)}) collective-permute-start(bf16[1,64,1,128]{3,1,2,0:T(8,128)(2,1)S(1)} %get-tuple-element.182), channel_id=1, source_target_pairs={{4,0},{5,1},{6,2},{7,3},{12,8},{13,9},{14,10},{15,11},{20,16},{21,... | collective-permute-start | bytes 49160 | tf_op jit(solution)/shard_map/ppermute | solution.py:17
  163.3 11.8 %collective-permute-start.38 = (bf16[1,64,1,128]{3,1,2,0:T(8,128)(2,1)S(1)}, bf16[1,64,1,128]{3,1,2,0:T(8,128)(2,1)S(1)}, u32[]{:S(2)}, u32[]{:S(2)}) collective-permute-start(bf16[1,64,1,128]{3,1,2,0:T(8,128)(2,1)S(1)} %get-tuple-element.181), channel_id=1, source_target_pairs={{0,4},{1,5},{2,6},{3,7},{8,12},{9,13},{10,14},{11,15},{16,20},{17,... | collective-permute-start | bytes 49160 | tf_op jit(solution)/shard_map/ppermute | solution.py:14
  169.5 17.2 %collective-permute-start.32 = (bf16[1,64,10,1]{3,1,2,0:T(8,128)(2,1)S(1)}, bf16[1,64,10,1]{3,1,2,0:T(8,128)(2,1)S(1)}, u32[]{:S(2)}, u32[]{:S(2)}) collective-permute-start(bf16[1,64,10,1]{3,1,2,0:T(8,128)(2,1)S(1)} %get-tuple-element.139), channel_id=1, source_target_pairs={{0,1},{1,2},{2,3},{4,5},{5,6},{6,7},{8,9},{9,10},{10,11},{12,13},{... | collective-permute-start | bytes 3848 | tf_op jit(solution)/shard_map/ppermute | solution.py:14
  171.4 15.3 %collective-permute-start.33 = (bf16[1,64,10,1]{3,1,2,0:T(8,128)(2,1)S(1)}, bf16[1,64,10,1]{3,1,2,0:T(8,128)(2,1)S(1)}, u32[]{:S(2)}, u32[]{:S(2)}) collective-permute-start(bf16[1,64,10,1]{3,1,2,0:T(8,128)(2,1)S(1)} %get-tuple-element.140), channel_id=1, source_target_pairs={{1,0},{2,1},{3,2},{5,4},{6,5},{7,6},{9,8},{10,9},{11,10},{13,12},{... | collective-permute-start | bytes 3848 | tf_op jit(solution)/shard_map/ppermute | solution.py:17
  298.4 12.5 %collective-permute-start.63 = (bf16[1,64,1,128]{3,1,2,0:T(8,128)(2,1)S(1)}, bf16[1,64,1,128]{3,1,2,0:T(8,128)(2,1)S(1)}, u32[]{:S(2)}, u32[]{:S(2)}) collective-permute-start(bf16[1,64,1,128]{3,1,2,0:T(8,128)(2,1)S(1)} %get-tuple-element.170), channel_id=1, source_target_pairs={{4,0},{5,1},{6,2},{7,3},{12,8},{13,9},{14,10},{15,11},{20,16},{21,... | collective-permute-start | bytes 49160 | tf_op jit(solution)/shard_map/ppermute | solution.py:17
  299.7 11.3 %collective-permute-start.62 = (bf16[1,64,1,128]{3,1,2,0:T(8,128)(2,1)S(1)}, bf16[1,64,1,128]{3,1,2,0:T(8,128)(2,1)S(1)}, u32[]{:S(2)}, u32[]{:S(2)}) collective-permute-start(bf16[1,64,1,128]{3,1,2,0:T(8,128)(2,1)S(1)} %get-tuple-element.169), channel_id=1, source_target_pairs={{0,4},{1,5},{2,6},{3,7},{8,12},{9,13},{10,14},{11,15},{16,20},{17,... | collective-permute-start | bytes 49160 | tf_op jit(solution)/shard_map/ppermute | solution.py:14
  349.6 10.8 %collective-permute-start = (f32[1,64,8,128]{3,2,1,0:T(8,128)S(1)}, f32[1,64,8,128]{3,2,1,0:T(8,128)S(1)}, u32[]{:S(2)}, u32[]{:S(2)}) collective-permute-start(f32[1,64,8,128]{3,2,1,0:T(8,128)S(1)} %multiply_add_fusion.4), channel_id=1, source_target_pairs={{0,8},{8,16},{16,24},{24,32},{32,40},{40,48},{48,56},{56,64},{64,7... | collective-permute-start | bytes 786440 | tf_op jit(solution)/shard_map/while/body/eval_jaxpr/ppermute | solution.py:25
  360.5 11.9 %collective-permute-start = (f32[1,64,8,128]{3,2,1,0:T(8,128)S(1)}, f32[1,64,8,128]{3,2,1,0:T(8,128)S(1)}, u32[]{:S(2)}, u32[]{:S(2)}) collective-permute-start(f32[1,64,8,128]{3,2,1,0:T(8,128)S(1)} %multiply_add_fusion.4), channel_id=1, source_target_pairs={{0,8},{8,16},{16,24},{24,32},{32,40},{40,48},{48,56},{56,64},{64,7... | collective-permute-start | bytes 786440 | tf_op jit(solution)/shard_map/while/body/eval_jaxpr/ppermute | solution.py:25
  372.6 13.1 %collective-permute-start = (f32[1,64,8,128]{3,2,1,0:T(8,128)S(1)}, f32[1,64,8,128]{3,2,1,0:T(8,128)S(1)}, u32[]{:S(2)}, u32[]{:S(2)}) collective-permute-start(f32[1,64,8,128]{3,2,1,0:T(8,128)S(1)} %multiply_add_fusion.4), channel_id=1, source_target_pairs={{0,8},{8,16},{16,24},{24,32},{32,40},{40,48},{48,56},{56,64},{64,7... | collective-permute-start | bytes 786440 | tf_op jit(solution)/shard_map/while/body/eval_jaxpr/ppermute | solution.py:25
  385.9 12.3 %collective-permute-start = (f32[1,64,8,128]{3,2,1,0:T(8,128)S(1)}, f32[1,64,8,128]{3,2,1,0:T(8,128)S(1)}, u32[]{:S(2)}, u32[]{:S(2)}) collective-permute-start(f32[1,64,8,128]{3,2,1,0:T(8,128)S(1)} %multiply_add_fusion.4), channel_id=1, source_target_pairs={{0,8},{8,16},{16,24},{24,32},{32,40},{40,48},{48,56},{56,64},{64,7... | collective-permute-start | bytes 786440 | tf_op jit(solution)/shard_map/while/body/eval_jaxpr/ppermute | solution.py:25
  398.4 11.5 %collective-permute-start = (f32[1,64,8,128]{3,2,1,0:T(8,128)S(1)}, f32[1,64,8,128]{3,2,1,0:T(8,128)S(1)}, u32[]{:S(2)}, u32[]{:S(2)}) collective-permute-start(f32[1,64,8,128]{3,2,1,0:T(8,128)S(1)} %multiply_add_fusion.4), channel_id=1, source_target_pairs={{0,8},{8,16},{16,24},{24,32},{32,40},{40,48},{48,56},{56,64},{64,7... | collective-permute-start | bytes 786440 | tf_op jit(solution)/shard_map/while/body/eval_jaxpr/ppermute | solution.py:25
  485.2 13.0 %collective-permute-start.1 = (f32[1,64,8,128]{3,2,1,0:T(8,128)S(1)}, f32[1,64,8,128]{3,2,1,0:T(8,128)S(1)}, u32[]{:S(2)}, u32[]{:S(2)}) collective-permute-start(f32[1,64,8,128]{3,2,1,0:T(8,128)S(1)} %multiply_add_fusion.5), channel_id=1, source_target_pairs={{8,0},{16,8},{24,16},{32,24},{40,32},{48,40},{56,48},{64,56},{72,6... | collective-permute-start | bytes 786440 | tf_op jit(solution)/shard_map/while/body/eval_jaxpr/ppermute | solution.py:25
  498.4 11.7 %collective-permute-start.1 = (f32[1,64,8,128]{3,2,1,0:T(8,128)S(1)}, f32[1,64,8,128]{3,2,1,0:T(8,128)S(1)}, u32[]{:S(2)}, u32[]{:S(2)}) collective-permute-start(f32[1,64,8,128]{3,2,1,0:T(8,128)S(1)} %multiply_add_fusion.5), channel_id=1, source_target_pairs={{8,0},{16,8},{24,16},{32,24},{40,32},{48,40},{56,48},{64,56},{72,6... | collective-permute-start | bytes 786440 | tf_op jit(solution)/shard_map/while/body/eval_jaxpr/ppermute | solution.py:25
  563.6 11.5 %collective-permute-start.1 = (f32[1,64,8,128]{3,2,1,0:T(8,128)S(1)}, f32[1,64,8,128]{3,2,1,0:T(8,128)S(1)}, u32[]{:S(2)}, u32[]{:S(2)}) collective-permute-start(f32[1,64,8,128]{3,2,1,0:T(8,128)S(1)} %multiply_add_fusion.5), channel_id=1, source_target_pairs={{8,0},{16,8},{24,16},{32,24},{40,32},{48,40},{56,48},{64,56},{72,6... | collective-permute-start | bytes 786440 | tf_op jit(solution)/shard_map/while/body/eval_jaxpr/ppermute | solution.py:25
  575.3 12.8 %collective-permute-start.1 = (f32[1,64,8,128]{3,2,1,0:T(8,128)S(1)}, f32[1,64,8,128]{3,2,1,0:T(8,128)S(1)}, u32[]{:S(2)}, u32[]{:S(2)}) collective-permute-start(f32[1,64,8,128]{3,2,1,0:T(8,128)S(1)} %multiply_add_fusion.5), channel_id=1, source_target_pairs={{8,0},{16,8},{24,16},{32,24},{40,32},{48,40},{56,48},{64,56},{72,6... | collective-permute-start | bytes 786440 | tf_op jit(solution)/shard_map/while/body/eval_jaxpr/ppermute | solution.py:25
  588.3 12.4 %collective-permute-start.1 = (f32[1,64,8,128]{3,2,1,0:T(8,128)S(1)}, f32[1,64,8,128]{3,2,1,0:T(8,128)S(1)}, u32[]{:S(2)}, u32[]{:S(2)}) collective-permute-start(f32[1,64,8,128]{3,2,1,0:T(8,128)S(1)} %multiply_add_fusion.5), channel_id=1, source_target_pairs={{8,0},{16,8},{24,16},{32,24},{40,32},{48,40},{56,48},{64,56},{72,6... | collective-permute-start | bytes 786440 | tf_op jit(solution)/shard_map/while/body/eval_jaxpr/ppermute | solution.py:25
  600.9 11.6 %collective-permute-start.1 = (f32[1,64,8,128]{3,2,1,0:T(8,128)S(1)}, f32[1,64,8,128]{3,2,1,0:T(8,128)S(1)}, u32[]{:S(2)}, u32[]{:S(2)}) collective-permute-start(f32[1,64,8,128]{3,2,1,0:T(8,128)S(1)} %multiply_add_fusion.5), channel_id=1, source_target_pairs={{8,0},{16,8},{24,16},{32,24},{40,32},{48,40},{56,48},{64,56},{72,6... | collective-permute-start | bytes 786440 | tf_op jit(solution)/shard_map/while/body/eval_jaxpr/ppermute | solution.py:25
  (93 other events, 647.6 us)
Sparse Core Ops, SparseCore 0:
  311.1 63.6 all-reduce.1
where the time goes:
time: 668 us; the launch traced here: 666 us
  starting transfers between devices  288 us (43%)
  waiting for transfers between devices  288 us (43%)
  matrix products  46.3 us (7%)
  between operations  17.3 us (3%)
  other arithmetic  16.5 us (2%)
  local copies, waits for them, and re-layouts  8.53 us (1%)
    ppermute x30, waiting for transfers between devices, passed_along(): lax.ppermute(value, axis, [(source, source + steps) for source in range(i...  207 us
    ppermute x30, starting transfers between devices, passed_along(): lax.ppermute(value, axis, [(source, source + steps) for source in range(i...  119 us
    ppermute x32, starting transfers between devices, with_halo(): lax.ppermute(lax.slice_in_dim(block, block.shape[dim] - width, None, axis...  103 us
    ppermute x32, starting transfers between devices, with_halo(): lax.ppermute(lax.slice_in_dim(block, 0, width, axis=dim), axis, backward)  65.8 us
    ppermute x32, waiting for transfers between devices, with_halo(): lax.ppermute(lax.slice_in_dim(block, 0, width, axis=dim), axis, backward)  44.8 us
    ppermute x32, waiting for transfers between devices, with_halo(): lax.ppermute(lax.slice_in_dim(block, block.shape[dim] - width, None, axis...  35.8 us
    dot_general x72, matrix products, convolve_back(): jnp.einsum('oc,bohw->bchw', kernel[tap_idx], window, preferred_element_ty...  18.3 us
    dot_general x72, matrix products, convolve(): jnp.einsum('oc,bchw->bohw', kernel[tap_idx], window, preferred_element_ty...  14 us
  transfers between devices with their start and end apart: 95, of which 65 were waited for; matrix products, arithmetic and copies ran while one was open for 5% of the time, Pallas kernels for 0%

commit v1 on v0

v1 whole, which is shorter than its diff:
```python
import jax
import jax.numpy as jnp
from jax import lax
from jax.experimental import pallas as pl
from jax.experimental.pallas import tpu as pltpu
from jax.sharding import PartitionSpec as P

HALO = 32
OWN = 64
BF = jnp.bfloat16
F32 = jnp.float32


def relax_kernel(x_ref, a_ref, w_ref, wt_ref, b_ref, phi_ref, psi_ref, g_ref, z_s, sl_s):
    blocks = w_ref.shape[0]
    strip = 2 * lax.axis_index("col") + lax.axis_index("row")
    strips = 2 * lax.axis_size("col")
    lane = lax.broadcasted_iota(jnp.int32, (64, 128), 1)
    column = strip * OWN - HALO + lane
    inside = jnp.where((column >= 0) & (column < strips * OWN), 1.0, 0.0).astype(F32)
    own = jnp.where((lane >= HALO) & (lane < HALO + OWN), 1.0, 0.0).astype(F32)
    phi_ref[...] = x_ref[...]
    psi_ref[...] = a_ref[...] * inside[None]
    zero = jnp.zeros((64, 128), BF)

    def forward(l, carry):
        w = w_ref[l]
        bias = b_ref[l]
        z_s[l, 0] = zero
        z_s[l, 17] = zero
        later, last = None, None
        for m in range(8):
            pieces = []
            for h in (2 * m, 2 * m + 1):
                t = jnp.tanh(phi_ref[h]) * inside
                sl_s[l, h] = inside - t * t
                z_s[l, h + 1] = (t * own).astype(BF)
                pieces.append(
                    jnp.concatenate(
                        [
                            pltpu.roll(t, 1, 1).astype(BF),
                            t.astype(BF),
                            pltpu.roll(t, 127, 1).astype(BF),
                        ],
                        axis=0,
                    )
                )
            rhs = jnp.concatenate(pieces, axis=1)
            prod = jnp.dot(w, rhs, preferred_element_type=F32)
            p0, p1 = prod[:, :128], prod[:, 128:]
            if m > 0:
                phi_ref[2 * m - 1] = phi_ref[2 * m - 1] + bias + (later + p0[128:])
                first = last + p0[64:128] + p1[128:]
            else:
                first = p0[64:128] + p1[128:]
            phi_ref[2 * m] = phi_ref[2 * m] + bias + first
            later = p0[:64] + p1[64:128]
            last = p1[:64]
        phi_ref[15] = phi_ref[15] + bias + later
        return carry

    lax.fori_loop(0, blocks, forward, 0)

    def backward(step, carry):
        l = blocks - 1 - step
        wt = wt_ref[l]
        grad = jnp.zeros((192, 192), F32)
        later, last = None, None
        for m in range(8):
            pieces = []
            zs = []
            for h in (2 * m, 2 * m + 1):
                a = psi_ref[h]
                pieces.append(
                    jnp.concatenate(
                        [
                            pltpu.roll(a, 127, 1).astype(BF),
                            a.astype(BF),
                            pltpu.roll(a, 1, 1).astype(BF),
                        ],
                        axis=0,
                    )
                )
                zs.append(jnp.concatenate([z_s[l, h], z_s[l, h + 1], z_s[l, h + 2]], axis=0))
            rhs = jnp.concatenate(pieces, axis=1)
            zz = jnp.concatenate(zs, axis=1)
            prod = jnp.dot(wt, rhs, preferred_element_type=F32)
            grad = grad + lax.dot_general(
                rhs, zz, (((1,), (1,)), ((), ())), preferred_element_type=F32
            )
            p0, p1 = prod[:, :128], prod[:, 128:]
            if m > 0:
                psi_ref[2 * m - 1] = psi_ref[2 * m - 1] + sl_s[l, 2 * m - 1] * (later + p0[:64])
                first = last + p0[64:128] + p1[:64]
            else:
                first = p0[64:128] + p1[:64]
            psi_ref[2 * m] = psi_ref[2 * m] + sl_s[l, 2 * m] * first
            later = p0[128:] + p1[64:128]
            last = p1[128:]
        psi_ref[15] = psi_ref[15] + sl_s[l, 15] * later
        g_ref[l] = 0.5 * grad
        return carry

    lax.fori_loop(0, blocks, backward, 0)


def relax(x, a, w, wt, b):
    blocks = w.shape[0]
    return pl.pallas_call(
        relax_kernel,
        out_shape=(
            jax.ShapeDtypeStruct((16, 64, 128), F32),
            jax.ShapeDtypeStruct((16, 64, 128), F32),
            jax.ShapeDtypeStruct((blocks, 192, 192), F32),
        ),
        in_specs=[pl.BlockSpec(memory_space=pltpu.VMEM)] * 5,
        out_specs=[pl.BlockSpec(memory_space=pltpu.VMEM)] * 3,
        scratch_shapes=[
            pltpu.VMEM((blocks, 18, 64, 128), BF),
            pltpu.VMEM((blocks, 16, 64, 128), F32),
        ],
        compiler_params=pltpu.CompilerParams(vmem_limit_bytes=48 << 20),
    )(x, a, w, wt, b)


def local(c_guess, adjoint_guess, weights, biases, coarse_gain):
    blocks = weights.shape[0]
    row = lax.axis_index("row")
    cols = lax.axis_size("col")
    both = jnp.stack([c_guess[0, 0], adjoint_guess[0, 0]])
    both = both.transpose(0, 2, 1, 3)
    full = lax.all_gather(both, "row", axis=1, tiled=True)
    perm = [(c, (c + 1) % cols) for c in range(cols)]
    perm += [(cols + c, cols + (c - 1) % cols) for c in range(cols)]
    low = row == 0
    edge = jnp.where(low, full[..., 128 - HALO :], full[..., :HALO])
    side = lax.ppermute(edge, ("row", "col"), perm)
    strip = jnp.where(
        low,
        jnp.concatenate([side, full[..., : 128 - HALO]], axis=-1),
        jnp.concatenate([full[..., HALO:], side], axis=-1),
    )
    taps = weights.reshape(blocks, 3, 3, 64, 64) * jnp.asarray(0.5, BF)
    w = taps.transpose(0, 1, 3, 2, 4).reshape(blocks, 192, 192)
    wt = taps.transpose(0, 1, 4, 2, 3).reshape(blocks, 192, 192)
    b = jnp.broadcast_to(0.5 * biases[:, :, None], (blocks, 64, 128))
    phi, psi, grad = relax(strip[0], strip[1], w, wt, b)
    grad = grad.reshape(blocks, 3, 64, 3, 64).transpose(0, 3, 1, 2, 4).reshape(blocks, 9, 64, 64)
    weight_grad = lax.psum(grad, ("row", "col"))

    index = lax.axis_index("layer")
    count = lax.axis_size("layer")
    gain = coarse_gain[0][None, :, None]
    core = slice(HALO, HALO + OWN)
    r = phi[..., core] - jnp.where(index == 0, 0.0, gain) * strip[0][..., core]
    s = psi[..., core] - jnp.where(index == count - 1, 0.0, gain) * strip[1][..., core]
    rs = jnp.concatenate([r, s], axis=-1)
    rs = lax.all_to_all(rs, "layer", 0, 0, tiled=True)
    gains = lax.all_gather(coarse_gain[0], "layer")[:, :, None]
    fwd = [jnp.zeros_like(rs[0, :, :OWN])]
    for d in range(count - 1):
        fwd.append(gains[d] * fwd[-1] + rs[d, :, :OWN])
    bwd = [jnp.zeros_like(rs[0, :, OWN:])]
    for d in range(count - 1, 0, -1):
        bwd.append(gains[d] * bwd[-1] + rs[d, :, OWN:])
    out = jnp.concatenate([jnp.stack(fwd), jnp.stack(bwd[::-1])], axis=-1)
    out = lax.all_to_all(out, "layer", 0, 0, tiled=True)
    out = out.reshape(16, 64, 2, OWN)
    out = lax.all_to_all(out, "row", 0, 3, tiled=True)
    c_states = out[:, :, 0].transpose(1, 0, 2)
    ends = out[:, :, 1].transpose(1, 0, 2)
    c_states = jnp.where(index == 0, c_guess[0, 0], c_states)
    ends = jnp.where(index == count - 1, adjoint_guess[0, 0], ends)
    return (c_states[None, None], ends[None, None], weight_grad)


def solution(mesh):
    in_specs = (
        P("layer", None, None, "row", "col"),
        P("layer", None, None, "row", "col"),
        P("layer", None, None, None),
        P("layer", None),
        P("layer", None),
    )
    out_specs = (
        P("layer", None, None, "row", "col"),
        P("layer", None, None, "row", "col"),
        P("layer", None, None, None),
    )
    return jax.shard_map(local, mesh=mesh, in_specs=in_specs, out_specs=out_specs, check_vma=False)
```

time: 668 us -> 190 us (0.28)
  the two profiles are of different devices: /device:TPU:104 before, /device:TPU:1 now
where the time goes in v1:
time: 190 us; the launch traced here: 188 us
  waiting for transfers between devices  78.6 us (41%)
  blocking collectives  31 us (16%)
  local copies, waits for them, and re-layouts  30 us (16%)
  between operations  14.4 us (8%)
  other arithmetic  14.1 us (7%)
  starting transfers between devices  11.2 us (6%)
  Pallas kernels  9.1 us (5%)
    psum x1, waiting for transfers between devices, local(): weight_grad = lax.psum(grad, ('row', 'col'))  51.4 us
    all_gather x1, waiting for transfers between devices, local(): full = lax.all_gather(both, 'row', axis=1, tiled=True)  20.2 us
    all_gather x1, blocking collectives, local(): gains = lax.all_gather(coarse_gain[0], 'layer')[:, :, None]  18.1 us
    all_to_all x1, blocking collectives, local(): out = lax.all_to_all(out, 'row', 0, 3, tiled=True)  12.8 us
    pallas_call x1, Pallas kernels, relax(): pl.pallas_call(relax_kernel, out_shape=(jax.ShapeDtypeStruct((16, 64, 128...  9.1 us
    all_to_all x1, starting transfers between devices, local(): rs = lax.all_to_all(rs, 'layer', 0, 0, tiled=True)  6.66 us
    unnamed x25, local copies, waits for them, and re-layouts  5.56 us
    ppermute x1, waiting for transfers between devices, local(): side = lax.ppermute(edge, ('row', 'col'), perm)  4.45 us
  transfers between devices with their start and end apart: 5, of which 4 were waited for; matrix products, arithmetic and copies ran while one was open for 13% of the time, Pallas kernels for 0%

profile of v1, /device:TPU:1, one launch (start us, length us, event | category | flops | bytes accessed | tf_op | source)
XLA Modules:
  0.0 188.4 jit_solution(2879598331680295922)
XLA Ops:
  7.2 1.2 copy_bitcast_fusion.2
  9.5 2.2 %copy.38 = bf16[8,3,3,64,64]{4,2,3,1,0:T(4,128)(2,1)} copy(bf16[8,3,3,64,64]{4,3,2,1,0:T(8,128)(2,1)S(1)} %bitcast.85) | data formatting | bytes 1179648 | tf_op jit(solution)/shard_map/mul | solution.py:143
  11.7 2.2 %copy.31 = bf16[8,3,3,64,64]{3,2,4,1,0:T(4,128)(2,1)} copy(bf16[8,3,3,64,64]{4,3,2,1,0:T(8,128)(2,1)S(1)} %bitcast.86) | data formatting | bytes 1179648 | tf_op jit(solution)/shard_map/mul | solution.py:143
  13.9 3.1 %reshape.1478.w_ref = bf16[8,192,192]{2,1,0:T(8,128)(2,1)S(1)} reshape(bf16[8,3,64,3,64]{4,3,2,1,0:T(4,128)(2,1)} %bitcast.89) | data formatting | bytes 1179648 | tf_op jit(solution)/shard_map/reshape | solution.py:144
  18.1 20.2 %all-gather.3.cloned.1.call-done = f32[2,16,64,128]{3,2,1,0:T(8,128)} async-done(((f32[2,8,64,128]{3,2,1,0:T(8,128)}), f32[2,16,64,128]{3,2,1,0:T(8,128)}) %all-gather.3.cloned.1.call-update) | async-done | bytes 1048592 | tf_op jit(solution)/shard_map/all_gather | solution.py:132
  38.3 2.9 %slice_select_fusion = f32[2,16,64,32]{3,2,1,0:T(8,128)} fusion(f32[2,16,64,128]{3,2,1,0:T(8,128)} %all-gather.3.cloned.1.call-done, pred[]{:T(512)S(6)} %eq.12), kind=kLoop, calls=%fused_computation.1 | loop fusion | flops 65536 | bytes 786433 | tf_op jit(solution)/shard_map/jit(_where)/select_n | solution.py:136
  41.1 1.6 copy.27
  43.7 1.7 fusion.10
  45.4 4.4 %collective-permute-done = f32[2,16,64,32]{2,3,1,0:T(8,128)} collective-permute-done((f32[2,16,64,32]{2,3,1,0:T(8,128)S(1)}, f32[2,16,64,32]{2,3,1,0:T(8,128)}, u32[]{:S(2)}, u32[]{:S(2)}) %collective-permute-start) | collective-permute-done | bytes 262176 | tf_op jit(solution)/shard_map/ppermute | solution.py:137
  49.8 2.4 %copy.28 = f32[2,16,64,32]{3,2,1,0:T(8,128)} copy(f32[2,16,64,32]{2,3,1,0:T(8,128)} %collective-permute-done) | data formatting | bytes 524288 | tf_op jit(solution)/shard_map/ppermute | solution.py:137
  52.2 2.8 %maximum_select_fusion = f32[2,16,64,128]{3,2,1,0:T(8,128)S(1)} fusion(f32[2,16,64,96]{3,2,1,0:T(8,128)} %get-tuple-element.34, f32[2,16,64,32]{3,2,1,0:T(8,128)} %copy.28, f32[2,16,64,96]{3,2,1,0:T(8,128)} %get-tuple-element.33, pred[]{:T(512)S(6)} %eq.12), kind=kLoop, calls=%fused_computation.2 | loop fusion | flops 786432 | bytes 2883585 | tf_op jit(solution)/shard_map/jit(_where)/select_n | solution.py:138
  55.2 9.1 %shard_map.76 = (f32[16,64,128]{2,1,0:T(8,128)S(1)}, f32[16,64,128]{2,1,0:T(8,128)S(1)}, f32[8,192,192]{2,1,0:T(8,128)S(1)}) custom-call(f32[16,64,128]{2,1,0:T(8,128)S(1)} %get-tuple-element.31.x_ref, f32[16,64,128]{2,1,0:T(8,128)S(1)} %get-tuple-element.32.a_ref, bf16[8,192,192]{2,1,0:T(8,128)(2,1)S(1)} %reshape.1478.w_ref, ...), custom_call_target="tpu_custom_call" | custom-call | tf_op jit(solution)/shard_map/pallas_call | solution.py:109
  66.0 6.7 %all-to-all-start = ((f32[16,64,128]{2,1,0:T(8,128)}), f32[16,64,128]{2,1,0:T(8,128)S(1)}, u32[]{:S(2)}, u32[]{:S(2)}) async-start(f32[16,64,128]{2,1,0:T(8,128)} %pad_maximum_fusion), calls=%async_computation | async-start | bytes 1048576 | tf_op jit(solution)/shard_map/all_to_all | solution.py:158
  72.7 18.1 %all-gather = f32[16,1,64]{2,1,0:T(1,128)S(1)} all-gather(f32[1,1,64]{2,1,0:T(1,128)S(1)} %bitcast.92), channel_id=1, replica_groups=mesh['layer'=16,'row'=2,'col'=4] {'layer'}, dimensions={0}, use_global_device_ids=true | all-gather | bytes 4352 | tf_op jit(solution)/shard_map/all_gather | solution.py:159
  92.6 1.0 pad_maximum_fusion.1
  93.6 3.6 %all-to-all-start.1 = ((f32[16,64,128]{2,1,0:T(8,128)}), f32[16,64,128]{2,1,0:T(8,128)S(1)}, u32[]{:S(2)}, u32[]{:S(2)}) async-start(f32[16,64,128]{2,1,0:T(8,128)} %pad_maximum_fusion.1), calls=%async_computation.1 | async-start | bytes 1048576 | tf_op jit(solution)/shard_map/all_to_all | solution.py:167
  97.3 2.7 %reshape.1481 = f32[8,3,64,3,64]{4,3,2,1,0:T(4,128)} reshape(f32[8,192,192]{2,1,0:T(8,128)S(1)} %get-tuple-element.8) | data formatting | bytes 2359296 | tf_op jit(solution)/shard_map/reshape | solution.py:148
  99.9 3.6 %copy.33 = f32[8,3,3,64,64]{4,3,2,1,0:T(8,128)} copy(f32[8,3,3,64,64]{4,1,3,2,0:T(4,128)} %bitcast.84) | data formatting | bytes 2359296 | tf_op jit(solution)/shard_map/transpose | solution.py:148
  103.6 2.5 %all-to-all-done.1 = f32[16,64,128]{2,1,0:T(8,128)S(1)} async-done(((f32[16,64,128]{2,1,0:T(8,128)}), f32[16,64,128]{2,1,0:T(8,128)S(1)}, u32[]{:S(2)}, u32[]{:S(2)}) %all-to-all-start.1) | async-done | bytes 524320 | tf_op jit(solution)/shard_map/all_to_all | solution.py:167
  106.7 1.2 reshape.1521
  107.9 12.8 %all_to_all.28 = f32[2,1,65536]{2,1,0:T(1,128)S(1)} all-to-all(f32[2,1,65536]{2,1,0:T(1,128)S(1)} %reshape.1521), channel_id=1, replica_groups=mesh['layer'=16,'row'=2,'col'=4] {'row'}, dimensions={0} | all-to-all | bytes 1048576 | tf_op jit(solution)/shard_map/all_to_all | solution.py:169
  121.2 2.3 %reduce = f32[2,65536]{1,0:T(2,128)S(1)} reduce(f32[2,1,65536]{2,1,0:T(1,128)S(1)} %all_to_all.28, f32[]{:T(128)} %broadcast.984), dimensions={1}, to_apply=%all_to_all.21.reduce_sub_computation | reduce | bytes 1048580 | tf_op jit(solution)/shard_map/all_to_all | solution.py:169
  126.8 51.4 %all-reduce.2.cloned.1.call-done = f32[8,9,64,64]{3,2,1,0:T(8,128)} async-done(((f32[8,9,64,64]{3,2,1,0:T(8,128)}), f32[8,9,64,64]{3,2,1,0:T(8,128)}) %all-reduce.2.cloned.1.call-update) | async-done | bytes 1179664 | tf_op jit(solution)/shard_map/psum | solution.py:149
  178.2 3.4 %copy.71 = f32[8,9,64,64]{3,2,1,0:T(8,128)} copy(f32[8,9,64,64]{3,2,1,0:T(8,128)} %all-reduce.2.cloned.1.call-done) | data formatting | bytes 2359296
  (62 shorter events, 10.9 us)
Async XLA Ops:
  7.2 2.2 %copy-start.2 = (bf16[8,9,64,64]{3,2,1,0:T(8,128)(2,1)S(1)}, bf16[8,9,64,64]{3,2,1,0:T(8,128)(2,1)}, u32[]{:S(2)}) copy-start(bf16[8,9,64,64]{3,2,1,0:T(8,128)(2,1)} %param.7) | copy-start | bytes 1769476
  7.2 31.1 %all-gather.3.cloned.1.call-start = ((), (), s32[]{:S(2)}) async-start(), calls=%async_computation.3 | async-start | bytes 1572864 | tf_op jit(solution)/shard_map/all_gather | solution.py:132
  13.9 3.2 %copy-start.1 = (bf16[8,3,3,64,64]{3,2,4,1,0:T(4,128)(2,1)S(1)}, bf16[8,3,3,64,64]{3,2,4,1,0:T(4,128)(2,1)}, u32[]{:S(2)}) copy-start(bf16[8,3,3,64,64]{3,2,4,1,0:T(4,128)(2,1)} %copy.31) | copy-start | bytes 1769476
  17.0 1.0 copy-start.6
  17.0 1.0 copy-start.5
  41.1 2.6 %copy-start = (f32[2,16,64,128]{3,2,1,0:T(8,128)S(1)}, f32[2,16,64,128]{3,2,1,0:T(8,128)}, u32[]{:S(2)}) copy-start(f32[2,16,64,128]{3,2,1,0:T(8,128)} %all-gather.3.cloned.1.call-done) | copy-start | bytes 3145732
  42.8 7.1 %collective-permute-start = (f32[2,16,64,32]{2,3,1,0:T(8,128)S(1)}, f32[2,16,64,32]{2,3,1,0:T(8,128)}, u32[]{:S(2)}, u32[]{:S(2)}) collective-permute-start(f32[2,16,64,32]{2,3,1,0:T(8,128)S(1)} %copy.27), channel_id=1, source_target_pairs={{0,1},{1,2},{2,3},{3,0},{4,7},{5,4},{6,5},{7,6},{8,9},{9,10},{10,1... | collective-permute-start | bytes 786440 | tf_op jit(solution)/shard_map/ppermute | solution.py:137
  66.0 24.8 %all-to-all-start = ((f32[16,64,128]{2,1,0:T(8,128)}), f32[16,64,128]{2,1,0:T(8,128)S(1)}, u32[]{:S(2)}, u32[]{:S(2)}) async-start(f32[16,64,128]{2,1,0:T(8,128)} %pad_maximum_fusion), calls=%async_computation | async-start | bytes 1048576 | tf_op jit(solution)/shard_map/all_to_all | solution.py:158
  93.6 12.5 %all-to-all-start.1 = ((f32[16,64,128]{2,1,0:T(8,128)}), f32[16,64,128]{2,1,0:T(8,128)S(1)}, u32[]{:S(2)}, u32[]{:S(2)}) async-start(f32[16,64,128]{2,1,0:T(8,128)} %pad_maximum_fusion.1), calls=%async_computation.1 | async-start | bytes 1048576 | tf_op jit(solution)/shard_map/all_to_all | solution.py:167
  97.2 81.0 %all-reduce.2.cloned.1.call-start = ((), (), s32[]{:S(2)}) async-start(), calls=%async_computation.4 | async-start | bytes 4718592 | tf_op jit(solution)/shard_map/psum | solution.py:149
  124.5 1.4 copy-start.3
  124.5 1.4 copy-start.4
Sparse Core Ops, SparseCore 0:
  9.7 28.5 all-gather.2
  103.7 74.4 all-reduce.1

commit v2 on v1

v2 whole, which is shorter than its diff:
```python
import jax
import jax.numpy as jnp
from jax import lax
from jax.experimental import pallas as pl
from jax.experimental.pallas import tpu as pltpu
from jax.sharding import PartitionSpec as P

HALO = 32
OWN = 64
BF = jnp.bfloat16
F32 = jnp.float32
MESH = pl.DeviceIdType.MESH


def remote(src, dst, send, recv, where):
    return pltpu.make_async_remote_copy(
        src_ref=src,
        dst_ref=dst,
        send_sem=send,
        recv_sem=recv,
        device_id=where,
        device_id_type=MESH,
    )


def fused_kernel(
    c_ref,
    a_ref,
    w_in,
    b_ref,
    gain_ref,
    pieces_out,
    grad_out,
    snd,
    rcv,
    edge_snd,
    edge_rcv,
    tmp,
    gain_snd,
    gain_rcv,
    gain_pk,
    gain_own,
    w_ref,
    wt_ref,
    b_s,
    phi_ref,
    psi_ref,
    z_s,
    sl_s,
    p1_snd,
    p1_rcv,
    p2_snd,
    p2_rcv,
    g_part,
    g_sib,
    g_half,
    g_chip,
    g_full,
    in_send,
    in_recv,
    gain_send,
    gain_recv,
    p1_send,
    p1_recv,
    p2_send,
    p2_recv,
    ga_send,
    ga_recv,
    gb_send,
    gb_recv,
    gc_send,
    gc_recv,
    gd_send,
    gd_recv,
):
    blocks = w_in.shape[0]
    layer = lax.axis_index("layer")
    row = lax.axis_index("row")
    col = lax.axis_index("col")
    layers = lax.axis_size("layer")
    cols = lax.axis_size("col")
    core = lax.rem(col, 2)
    chip = 2 * row + col // 2
    strip = 2 * col + row
    lane = lax.broadcasted_iota(jnp.int32, (64, 128), 1)
    lane32 = lax.broadcasted_iota(jnp.int32, (32, 128), 1)
    lane16 = lax.broadcasted_iota(jnp.int32, (16, 128), 1)
    column = strip * OWN - HALO + lane
    inside = jnp.where((column >= 0) & (column < 2 * cols * OWN), 1.0, 0.0).astype(F32)
    own = jnp.where((lane >= HALO) & (lane < HALO + OWN), 1.0, 0.0).astype(F32)
    top = row == 0

    barrier = pltpu.get_barrier_semaphore()

    def greet(n, carry):
        e, rho = n // 2, lax.rem(n, 2)

        @pl.when(jnp.logical_or(e != layer, rho != row))
        def _():
            pl.semaphore_signal(
                barrier, inc=1, device_id={"layer": e, "row": rho}, device_id_type=MESH
            )

        return carry

    lax.fori_loop(0, 2 * layers, greet, 0)
    for step in range(1, cols):
        for rho in range(2):
            pl.semaphore_signal(
                barrier,
                inc=1,
                device_id={"row": rho, "col": lax.rem(col + step, cols)},
                device_id_type=MESH,
            )

    def pack(src, n):
        def one(h, carry):
            x = src[pl.ds(h, 64, stride=8), :]
            snd[n, h] = x.astype(BF)
            for side in range(2):
                edge = jnp.zeros((16, 128), F32)
                for g in range(4):
                    part = x[16 * g : 16 * g + 16]
                    shift = (32 * g + (32 if side == 0 else 0)) % 128
                    if shift:
                        part = pltpu.roll(part, shift, 1)
                    edge = jnp.where(lane16 // 32 == g, part, edge)
                edge_snd[side, n, h] = edge.astype(BF)
            return carry

        lax.fori_loop(0, 8, one, 0)

    def exchange(n):
        yield remote(snd.at[n], rcv.at[n], in_send.at[n, 0], in_recv.at[n, 0], {"row": 1 - row})
        yield remote(
            edge_snd.at[0, n],
            edge_rcv.at[row, n],
            in_send.at[n, 1],
            in_recv.at[n, 1 + row],
            {"row": 0, "col": lax.rem(col + 1, cols)},
        )
        yield remote(
            edge_snd.at[1, n],
            edge_rcv.at[row, n],
            in_send.at[n, 2],
            in_recv.at[n, 1 + row],
            {"row": 1, "col": lax.rem(col + cols - 1, cols)},
        )

    def arrived(n):
        remote(snd.at[n], rcv.at[n], in_send.at[n, 0], in_recv.at[n, 0], {"row": 1 - row}).wait_recv()
        for rho in range(2):
            remote(
                edge_snd.at[0, n],
                edge_rcv.at[rho, n],
                in_send.at[n, 1],
                in_recv.at[n, 1 + rho],
                {"row": 1 - row},
            ).wait_recv()

    pack(c_ref, 0)
    pl.semaphore_wait(barrier, 2 * layers - 1 + 2 * (cols - 1))
    for copy in exchange(0):
        copy.start()
    pack(a_ref, 1)
    for copy in exchange(1):
        copy.start()

    def lay_weights(l, carry):
        for i in range(3):
            w_ref[l, 64 * i : 64 * i + 64, :] = jnp.concatenate(
                [w_in[l, 3 * i + j] * jnp.asarray(0.5, BF) for j in range(3)], axis=1
            )
            stack = w_in[l, 3 * i : 3 * i + 3].reshape(192, 64)
            wt_ref[l, 64 * i : 64 * i + 64, :] = (0.5 * stack.astype(F32)).T.astype(BF)
        return carry

    lax.fori_loop(0, blocks, lay_weights, 0)
    tmp[...] = jnp.zeros_like(tmp)
    tmp[0:blocks, 0:64] = 0.5 * b_ref[...]
    tmp[blocks : blocks + 1, 0:64] = gain_ref[...]
    turned = tmp[...].T
    for l in range(blocks):
        b_s[l] = jnp.broadcast_to(turned[0:64, l : l + 1], (64, 128))
    gain_own[...] = jnp.broadcast_to(turned[0:64, blocks : blocks + 1], (64, 128))
    gain_snd[...] = tmp[blocks : blocks + 8, :]

    def holder(h):
        return 2 * lax.rem(h, 8) + row, h // 8

    def stays(h):
        lam, rho = holder(h)
        return jnp.logical_and(lam == layer, rho == row)

    def gain_copy(h):
        lam, rho = holder(h)
        return remote(
            gain_snd,
            gain_rcv.at[layer],
            gain_send.at[h],
            gain_recv.at[layer],
            {"layer": lam, "row": rho},
        )

    def p1_copy(n, h):
        lam, rho = holder(h)
        return remote(
            p1_snd.at[n, h],
            p1_rcv.at[n, layer],
            p1_send.at[n, h],
            p1_recv.at[n, layer],
            {"layer": lam, "row": rho},
        )

    def comes(e):
        return jnp.logical_or(e != layer, lax.rem(layer, 2) != row)

    def send_gain(h, carry):
        @pl.when(stays(h))
        def _():
            gain_rcv[layer] = gain_snd[...]

        @pl.when(jnp.logical_not(stays(h)))
        def _():
            gain_copy(h).start()

        return carry

    lax.fori_loop(0, 16, send_gain, 0)

    def assemble(src, n, dst):
        shift = jnp.where(top, 32, 96)

        def halo(rho, h):
            packed = edge_rcv[rho, n, h].astype(F32)
            return jnp.concatenate(
                [
                    pltpu.roll(packed, jnp.where(top, (128 - 32 * g) % 128, (96 - 32 * g) % 128), 1)
                    for g in range(4)
                ],
                axis=0,
            )

        start = jnp.where(top, 0, 96)
        outer = (lane >= start) & (lane < start + 32)

        def one(h, carry):
            x = src[pl.ds(h, 64, stride=8), :]
            dst[8 * row + h] = jnp.where(outer, halo(row, h), pltpu.roll(x, shift, 1)) * inside
            y = rcv[n, h].astype(F32)
            dst[8 * (1 - row) + h] = (
                jnp.where(outer, halo(1 - row, h), pltpu.roll(y, shift, 1)) * inside
            )
            return carry

        lax.fori_loop(0, 8, one, 0)

    arrived(0)
    assemble(c_ref, 0, phi_ref)

    zero = jnp.zeros((64, 128), BF)

    def forward(l, carry):
        w = w_ref[l]
        bias = b_s[l]
        z_s[l, 0] = zero
        z_s[l, 17] = zero
        later, last = None, None
        for m in range(8):
            pieces = []
            for h in (2 * m, 2 * m + 1):
                t = jnp.tanh(phi_ref[h]) * inside
                sl_s[l, h] = inside - t * t
                z_s[l, h + 1] = (t * own).astype(BF)
                pieces.append(
                    jnp.concatenate(
                        [
                            pltpu.roll(t, 1, 1).astype(BF),
                            t.astype(BF),
                            pltpu.roll(t, 127, 1).astype(BF),
                        ],
                        axis=0,
                    )
                )
            rhs = jnp.concatenate(pieces, axis=1)
            prod = jnp.dot(w, rhs, preferred_element_type=F32)
            p0, p1 = prod[:, :128], prod[:, 128:]
            if m > 0:
                phi_ref[2 * m - 1] = phi_ref[2 * m - 1] + bias + (later + p0[128:])
                first = last + p0[64:128] + p1[128:]
            else:
                first = p0[64:128] + p1[128:]
            phi_ref[2 * m] = phi_ref[2 * m] + bias + first
            later = p0[:64] + p1[64:128]
            last = p1[:64]
        phi_ref[15] = phi_ref[15] + bias + later
        return carry

    lax.fori_loop(0, blocks, forward, 0)

    def send_pieces(n, field, guess_own, keep):
        gain = gain_own[...] * keep
        shift = jnp.where(top, 32, 96)

        def one(h, carry):
            rho, u = h // 8, lax.rem(h, 8)
            mine = pltpu.roll(guess_own[pl.ds(u, 64, stride=8), :], shift, 1)
            other = pltpu.roll(rcv[n, u].astype(F32), shift, 1)
            here = jnp.where(rho == row, 1.0, 0.0)
            r = field[h] - gain * (here * mine + (1.0 - here) * other)
            packed = jnp.where(lane32 < 64, pltpu.roll(r[:32], 96, 1), pltpu.roll(r[32:], 32, 1))

            @pl.when(stays(h))
            def _():
                p1_rcv[n, layer] = packed.astype(BF)

            @pl.when(jnp.logical_not(stays(h)))
            def _():
                p1_snd[n, h] = packed.astype(BF)
                p1_copy(n, h).start()

            return carry

        lax.fori_loop(0, 16, one, 0)

    def p2_copy(n, e):
        return remote(
            p2_snd.at[n, e],
            p2_rcv.at[n, layer],
            p2_send.at[n, e],
            p2_recv.at[n, layer],
            {"layer": e},
        )

    def solve(n):
        first = 0 if n == 0 else layers - 1
        stride = 1 if n == 0 else -1

        def one(k, state):
            e = first + stride * k

            @pl.when(comes(e))
            def _():
                remote(
                    p1_snd.at[n, 0],
                    p1_rcv.at[n, e],
                    p1_send.at[n, 0],
                    p1_recv.at[n, e],
                    {"layer": layer, "row": 1 - row},
                ).wait_recv()

            state = gain_pk[e] * state + p1_rcv[n, e].astype(F32)
            target = e + stride

            @pl.when(target == layer)
            def _():
                p2_rcv[n, layer] = state.astype(BF)

            @pl.when(target != layer)
            def _():
                p2_snd[n, target] = state.astype(BF)
                p2_copy(n, target).start()

            return state

        lax.fori_loop(0, layers - 1, one, jnp.zeros((32, 128), F32))
        unused = layers - 1 if n == 0 else 0

        @pl.when(comes(unused))
        def _():
            remote(
                p1_snd.at[n, 0],
                p1_rcv.at[n, unused],
                p1_send.at[n, 0],
                p1_recv.at[n, unused],
                {"layer": layer, "row": 1 - row},
            ).wait_recv()

    send_pieces(0, phi_ref, c_ref, jnp.where(layer == 0, 0.0, 1.0))

    def take_gain(e, carry):
        @pl.when(comes(e))
        def _():
            remote(
                gain_snd,
                gain_rcv.at[e],
                gain_send.at[0],
                gain_recv.at[e],
                {"layer": layer, "row": 1 - row},
            ).wait_recv()

        return carry

    lax.fori_loop(0, layers, take_gain, 0)
    for e in range(16):
        tmp[e : e + 1, :] = gain_rcv[e, 0:1, :]
    turned_all = tmp[...].T
    for e in range(16):
        gain_pk[e] = jnp.where(
            lane32 < 64,
            jnp.broadcast_to(turned_all[0:32, e : e + 1], (32, 128)),
            jnp.broadcast_to(turned_all[32:64, e : e + 1], (32, 128)),
        )

    half = pl.ds(pl.multiple_of(144 * core, 16), 144)
    other_half = pl.ds(pl.multiple_of(144 * (1 - core), 16), 144)
    beside = {"col": col + 1 - 2 * core}

    def ga_copy(l):
        return remote(g_part.at[l, other_half], g_sib.at[l], ga_send.at[l], ga_recv.at[l], beside)

    def at_chip(y):
        return {"row": y // 2, "col": 2 * lax.rem(y, 2) + core}

    def gb_copy(l):
        y = lax.rem(l, 4)
        return remote(
            g_half.at[l],
            g_chip.at[l // 4, chip],
            gb_send.at[l],
            gb_recv.at[l // 4, chip],
            at_chip(y),
        )

    def gc_copy(l, step):
        y = lax.rem(chip + step, 4)
        return remote(
            g_full.at[l, half],
            g_full.at[l, half],
            gc_send.at[l // 4, step - 1],
            gc_recv.at[l],
            at_chip(y),
        )

    def gd_copy(l):
        return remote(g_full.at[l, half], g_full.at[l, half], gd_send.at[l], gd_recv.at[l], beside)

    def to_owner(l):
        ga_copy(l).wait_recv()
        total = (g_part[l, half, :] + g_sib[l]).astype(BF)

        @pl.when(lax.rem(l, 4) == chip)
        def _():
            g_chip[l // 4, chip] = total

        @pl.when(lax.rem(l, 4) != chip)
        def _():
            g_half[l] = total
            gb_copy(l).start()

    def own_block(q):
        l = 4 * q + chip
        for step in range(1, 4):
            y = lax.rem(chip + step, 4)
            remote(
                g_half.at[l],
                g_chip.at[q, y],
                gb_send.at[l],
                gb_recv.at[q, y],
                at_chip(y),
            ).wait_recv()
        total = g_chip[q, 0].astype(F32) + g_chip[q, 1].astype(F32)
        total = total + g_chip[q, 2].astype(F32) + g_chip[q, 3].astype(F32)
        g_full[l, half, :] = total.astype(BF)
        for step in range(1, 4):
            gc_copy(l, step).start()

    arrived(1)
    assemble(a_ref, 1, psi_ref)

    def backward(step, carry):
        l = blocks - 1 - step
        wt = wt_ref[l]
        grad = jnp.zeros((192, 192), F32)
        later, last = None, None
        for m in range(8):
            pieces = []
            zs = []
            for h in (2 * m, 2 * m + 1):
                a = psi_ref[h]
                pieces.append(
                    jnp.concatenate(
                        [
                            pltpu.roll(a, 127, 1).astype(BF),
                            a.astype(BF),
                            pltpu.roll(a, 1, 1).astype(BF),
                        ],
                        axis=0,
                    )
                )
                zs.append(jnp.concatenate([z_s[l, h], z_s[l, h + 1], z_s[l, h + 2]], axis=0))
            rhs = jnp.concatenate(pieces, axis=1)
            zz = jnp.concatenate(zs, axis=1)
            prod = jnp.dot(wt, rhs, preferred_element_type=F32)
            grad = grad + lax.dot_general(
                rhs, zz, (((1,), (1,)), ((), ())), preferred_element_type=F32
            )
            p0, p1 = prod[:, :128], prod[:, 128:]
            if m > 0:
                psi_ref[2 * m - 1] = psi_ref[2 * m - 1] + sl_s[l, 2 * m - 1] * (later + p0[:64])
                first = last + p0[64:128] + p1[:64]
            else:
                first = p0[64:128] + p1[:64]
            psi_ref[2 * m] = psi_ref[2 * m] + sl_s[l, 2 * m] * first
            later = p0[128:] + p1[64:128]
            last = p1[128:]
        psi_ref[15] = psi_ref[15] + sl_s[l, 15] * later
        grad = 0.5 * grad
        g_part[l, 0:192, :] = grad[:, :128]
        g_part[l, 192:288, 0:64] = grad[:96, 128:192]
        g_part[l, 192:288, 64:128] = grad[96:, 128:192]
        ga_copy(l).start()

        @pl.when(step >= 2)
        def _():
            to_owner(l + 2)

        @pl.when(step == 5)
        def _():
            solve(0)

        return carry

    lax.fori_loop(0, blocks, backward, 0)

    send_pieces(1, psi_ref, a_ref, jnp.where(layer == layers - 1, 0.0, 1.0))
    own_block(1)
    to_owner(1)
    to_owner(0)
    solve(1)
    own_block(0)

    def forward_half(k, carry):
        l = blocks - 1 - k

        @pl.when(lax.rem(l, 4) != chip)
        def _():
            remote(
                g_full.at[l, half],
                g_full.at[l, half],
                gc_send.at[0, 0],
                gc_recv.at[l],
                at_chip(lax.rem(l, 4)),
            ).wait_recv()

        gd_copy(l).start()
        return carry

    lax.fori_loop(0, blocks, forward_half, 0)

    for n in range(2):
        for copy in exchange(n):
            copy.wait_send()

    def drain(h, carry):
        @pl.when(jnp.logical_not(stays(h)))
        def _():
            gain_copy(h).wait_send()
            for n in range(2):
                p1_copy(n, h).wait_send()

        for n in range(2):
            skipped = 0 if n == 0 else layers - 1

            @pl.when(jnp.logical_and(h != layer, h != skipped))
            def _():
                p2_copy(n, h).wait_send()

            @pl.when(jnp.logical_and(h != layer, layer != skipped))
            def _():
                remote(
                    p2_snd.at[n, 0],
                    p2_rcv.at[n, h],
                    p2_send.at[n, 0],
                    p2_recv.at[n, h],
                    {"row": 1 - row},
                ).wait_recv()

        return carry

    lax.fori_loop(0, 16, drain, 0)

    def drain_grads(l, carry):
        ga_copy(l).wait_send()

        @pl.when(lax.rem(l, 4) != chip)
        def _():
            gb_copy(l).wait_send()

        gd_copy(l).wait_send()
        remote(
            g_full.at[l, other_half],
            g_full.at[l, other_half],
            gd_send.at[l],
            gd_recv.at[l],
            beside,
        ).wait_recv()
        return carry

    lax.fori_loop(0, blocks, drain_grads, 0)
    for q in range(2):
        for step in range(1, 4):
            gc_copy(4 * q + chip, step).wait_send()
    for n in range(2):

        @pl.when(layer != (0 if n == 0 else layers - 1))
        def _():
            pieces_out[n] = p2_rcv[n]

    grad_out[...] = g_full[...]


def fused(c, a, w, b, gain):
    blocks = w.shape[0]
    vm = pltpu.VMEM
    dma = pltpu.SemaphoreType.DMA
    return pl.pallas_call(
        fused_kernel,
        out_shape=(
            jax.ShapeDtypeStruct((2, 16, 32, 128), BF),
            jax.ShapeDtypeStruct((blocks, 288, 128), BF),
        ),
        in_specs=[pl.BlockSpec(memory_space=vm)] * 5,
        out_specs=[pl.BlockSpec(memory_space=vm)] * 2,
        scratch_shapes=[
            vm((2, 8, 64, 128), BF),
            vm((2, 8, 64, 128), BF),
            vm((2, 2, 8, 16, 128), BF),
            vm((2, 2, 8, 16, 128), BF),
            vm((128, 128), F32),
            vm((8, 128), F32),
            vm((16, 8, 128), F32),
            vm((16, 32, 128), F32),
            vm((64, 128), F32),
            vm((blocks, 192, 192), BF),
            vm((blocks, 192, 192), BF),
            vm((blocks, 64, 128), F32),
            vm((16, 64, 128), F32),
            vm((16, 64, 128), F32),
            vm((blocks, 18, 64, 128), BF),
            vm((blocks, 16, 64, 128), F32),
            vm((2, 16, 32, 128), BF),
            vm((2, 16, 32, 128), BF),
            vm((2, 16, 32, 128), BF),
            vm((2, 16, 32, 128), BF),
            vm((blocks, 288, 128), F32),
            vm((blocks, 144, 128), F32),
            vm((blocks, 144, 128), BF),
            vm((2, 4, 144, 128), BF),
            vm((blocks, 288, 128), BF),
            dma((2, 3)),
            dma((2, 3)),
            dma((16,)),
            dma((16,)),
            dma((2, 16)),
            dma((2, 16)),
            dma((2, 16)),
            dma((2, 16)),
            dma((blocks,)),
            dma((blocks,)),
            dma((blocks,)),
            dma((2, 4)),
            dma((2, 3)),
            dma((blocks,)),
            dma((blocks,)),
            dma((blocks,)),
        ],
        compiler_params=pltpu.CompilerParams(
            vmem_limit_bytes=48 << 20, collective_id=0, has_side_effects=True
        ),
    )(c, a, w, b, gain)


def unpack_kernel(c_ref, a_ref, pieces_ref, grad_ref, c_out, a_out, g_out):
    layer = lax.axis_index("layer")
    layers = lax.axis_size("layer")
    lane32 = lax.broadcasted_iota(jnp.int32, (32, 128), 1)

    @pl.when(pl.program_id(0) == 0)
    def _():
        for n, src, dst, skipped in ((0, c_ref, c_out, 0), (1, a_ref, a_out, layers - 1)):

            @pl.when(layer == skipped)
            def _():
                dst[...] = src[...]

            @pl.when(layer != skipped)
            def _():
                for u in range(8):
                    left = pieces_ref[n, 2 * u].astype(F32)
                    right = pieces_ref[n, 2 * u + 1].astype(F32)
                    dst[pl.ds(u, 32, stride=8), :] = jnp.where(
                        lane32 < 64, left, pltpu.roll(right, 64, 1)
                    )
                    dst[pl.ds(256 + u, 32, stride=8), :] = jnp.where(
                        lane32 < 64, pltpu.roll(left, 64, 1), right
                    )

    for j in range(3):
        g_out[0, j] = grad_ref[0, 64 * j : 64 * j + 64, 0:64].astype(F32)
        g_out[0, 3 + j] = grad_ref[0, 64 * j : 64 * j + 64, 64:128].astype(F32)
    g_out[0, 6] = grad_ref[0, 192:256, 0:64].astype(F32)
    g_out[0, 7, 0:32] = grad_ref[0, 256:288, 0:64].astype(F32)
    g_out[0, 7, 32:64] = grad_ref[0, 192:224, 64:128].astype(F32)
    g_out[0, 8] = grad_ref[0, 224:288, 64:128].astype(F32)


def unpack(c, a, pieces, grad):
    blocks = grad.shape[0]
    whole = pl.BlockSpec((512, 128), lambda l: (0, 0))
    return pl.pallas_call(
        unpack_kernel,
        grid=(blocks,),
        out_shape=(
            jax.ShapeDtypeStruct((512, 128), F32),
            jax.ShapeDtypeStruct((512, 128), F32),
            jax.ShapeDtypeStruct((blocks, 9, 64, 64), F32),
        ),
        in_specs=[
            whole,
            whole,
            pl.BlockSpec((2, 16, 32, 128), lambda l: (0, 0, 0, 0)),
            pl.BlockSpec((1, 288, 128), lambda l: (l, 0, 0)),
        ],
        out_specs=[whole, whole, pl.BlockSpec((1, 9, 64, 64), lambda l: (l, 0, 0, 0))],
        compiler_params=pltpu.CompilerParams(vmem_limit_bytes=32 << 20),
    )(c, a, pieces, grad)


def local(c_guess, adjoint_guess, weights, biases, coarse_gain):
    c = c_guess.reshape(512, 128)
    a = adjoint_guess.reshape(512, 128)
    pieces, grad = fused(c, a, weights, biases, coarse_gain)
    c_states, ends, weight_grad = unpack(c, a, pieces, grad)
    return (c_states.reshape(c_guess.shape), ends.reshape(c_guess.shape), weight_grad)


def solution(mesh):
    in_specs = (
        P("layer", None, None, "row", "col"),
        P("layer", None, None, "row", "col"),
        P("layer", None, None, None),
        P("layer", None),
        P("layer", None),
    )
    out_specs = (
        P("layer", None, None, "row", "col"),
        P("layer", None, None, "row", "col"),
        P("layer", None, None, None),
    )
    return jax.shard_map(local, mesh=mesh, in_specs=in_specs, out_specs=out_specs, check_vma=False)
```

time: 190 us -> 55.5 us (0.29)
  waiting for transfers between devices: 78.6 us -> 0 us
  Pallas kernels: 9.1 us -> 50.1 us
  blocking collectives: 31 us -> 0 us
  local copies, waits for them, and re-layouts: 30 us -> 4.5 us
  other arithmetic: 14.1 us -> 0 us
  between operations: 14.4 us -> 0.65 us
  starting transfers between devices: 11.2 us -> 0 us
    psum x1 -> x0, waiting for transfers between devices: 51.4 us -> none  [local(): weight_grad = lax.psum(grad, ('row', 'col'))]
    pallas_call x1 -> x2, Pallas kernels: 9.1 us -> 50.1 us  [the longest x1 46.4 us: fused(): pl.pallas_call(fused_kernel, out_shape=(jax.ShapeDtypeStruct((2, 16, 32,...]
    all_gather x1 -> x0, waiting for transfers between devices: 20.2 us -> none  [local(): full = lax.all_gather(both, 'row', axis=1, tiled=True)]
    all_gather x1 -> x0, blocking collectives: 18.1 us -> none  [local(): gains = lax.all_gather(coarse_gain[0], 'layer')[:, :, None]]
    all_to_all x1 -> x0, blocking collectives: 12.8 us -> none  [local(): out = lax.all_to_all(out, 'row', 0, 3, tiled=True)]
    all_to_all x2 -> x0, starting transfers between devices: 10.2 us -> none  [the longest x1 6.66 us: local(): rs = lax.all_to_all(rs, 'layer', 0, 0, tiled=True)]
    reshape x4 -> x0, local copies, waits for them, and re-layouts: 7.36 us -> none  [the longest x1 3.12 us: local(): w = taps.transpose(0, 1, 3, 2, 4).reshape(blocks, 192, 192)]
    select_n x3 -> x0, other arithmetic: 5.64 us -> none  [the longest x1 2.86 us: local(): edge = jnp.where(low, full[..., 128 - HALO:], full[..., :HALO])]
  transfers between devices with their start and end apart: 5 -> 0, of which waited for: 4 -> 0; matrix products, arithmetic and copies ran while one was open for 13% -> 0% of each run, Pallas kernels for 0% -> 0%
where the time goes in v2:
time: 55.5 us; the launch traced here: 55.3 us
  Pallas kernels  50.1 us (90%)
  local copies, waits for them, and re-layouts  4.5 us (8%)
  between operations  0.65 us (1%)
    pallas_call x1, Pallas kernels, fused(): pl.pallas_call(fused_kernel, out_shape=(jax.ShapeDtypeStruct((2, 16, 32,...  46.4 us
    unnamed x10, local copies, waits for them, and re-layouts  4.5 us
    pallas_call x1, Pallas kernels, unpack(): pl.pallas_call(unpack_kernel, grid=(blocks,), out_shape=(jax.ShapeDtypeSt...  3.67 us

profile of v2, /device:TPU:1, one launch (start us, length us, event | category | flops | bytes accessed | tf_op | source)
XLA Modules:
  0.0 55.3 jit_solution(3512104072949578717)
XLA Ops:
  0.6 0.0 copy-start
  0.6 1.3 %copy-done = bf16[8,9,64,64]{3,2,1,0:T(8,128)(2,1)S(1)} copy-done((bf16[8,9,64,64]{3,2,1,0:T(8,128)(2,1)S(1)}, bf16[8,9,64,64]{3,2,1,0:T(8,128)(2,1)}, u32[]{:S(2)}) %copy-start) | copy-done | bytes 589848
  1.9 0.0 copy-start.1
  1.9 0.9 %copy-done.1 = f32[1,1,64,8,128]{4,3,2,1,0:T(8,128)S(1)} copy-done((f32[1,1,64,8,128]{4,3,2,1,0:T(8,128)S(1)}, f32[1,1,64,8,128]{4,3,2,1,0:T(8,128)}, u32[]{:S(2)}) %copy-start.1) | copy-done | bytes 262168
  2.9 0.0 copy-start.2
  2.9 0.9 %copy-done.2 = f32[1,1,64,8,128]{4,3,2,1,0:T(8,128)S(1)} copy-done((f32[1,1,64,8,128]{4,3,2,1,0:T(8,128)S(1)}, f32[1,1,64,8,128]{4,3,2,1,0:T(8,128)}, u32[]{:S(2)}) %copy-start.2) | copy-done | bytes 262168
  3.8 0.0 copy-start.3
  3.8 0.7 %copy-done.3 = f32[8,64]{1,0:T(8,128)S(1)} copy-done((f32[8,64]{1,0:T(8,128)S(1)}, f32[8,64]{1,0:T(8,128)}, u32[]{:S(2)}) %copy-start.3) | copy-done | bytes 2072
  4.5 0.0 copy-start.4
  4.5 0.7 %copy-done.4 = f32[1,64]{1,0:T(1,128)S(1)} copy-done((f32[1,64]{1,0:T(1,128)S(1)}, f32[1,64]{1,0:T(1,128)}, u32[]{:S(2)}) %copy-start.4) | copy-done | bytes 280
  5.1 46.4 %shard_map.76 = (bf16[2,16,32,128]{3,2,1,0:T(8,128)(2,1)S(1)}, bf16[8,288,128]{2,1,0:T(8,128)(2,1)S(1)}) custom-call(f32[512,128]{1,0:T(8,128)S(1)} %bitcast.4, f32[512,128]{1,0:T(8,128)S(1)} %bitcast.6, bf16[8,9,64,64]{3,2,1,0:T(8,128)(2,1)S(1)} %copy-done, f32[8,64]{1,0:T(8,128)S(1)} %copy-done.3, f32[1,64]{1,0:T(1,128)S(1)} %copy-done.4), custom_call_target="tpu_custom_call" | custom-call | tf_op jit(solution)/shard_map/pallas_call | solution.py:617
  51.6 3.7 %shard_map.77 = (f32[512,128]{1,0:T(8,128)}, f32[512,128]{1,0:T(8,128)}, f32[8,9,64,64]{3,2,1,0:T(8,128)}) custom-call(f32[512,128]{1,0:T(8,128)S(1)} %bitcast.5, f32[512,128]{1,0:T(8,128)S(1)} %bitcast.7, bf16[2,16,32,128]{3,2,1,0:T(8,128)(2,1)S(1)} %get-tuple-element.8.pieces_ref, bf16[8,288,128]{2,1,0:T(8,128)(2,1)S(1)} %get-tuple-element.9.grad_ref), custom_call_target="tpu_custom_call" | custom-call | tf_op jit(solution)/shard_map/pallas_call | solution.py:711
Async XLA Ops:
  0.6 1.3 %copy-start = (bf16[8,9,64,64]{3,2,1,0:T(8,128)(2,1)S(1)}, bf16[8,9,64,64]{3,2,1,0:T(8,128)(2,1)}, u32[]{:S(2)}) copy-start(bf16[8,9,64,64]{3,2,1,0:T(8,128)(2,1)} %w_in.1) | copy-start | bytes 1769476
  1.9 0.9 %copy-start.1 = (f32[1,1,64,8,128]{4,3,2,1,0:T(8,128)S(1)}, f32[1,1,64,8,128]{4,3,2,1,0:T(8,128)}, u32[]{:S(2)}) copy-start(f32[1,1,64,8,128]{4,3,2,1,0:T(8,128)} %param.5) | copy-start | bytes 786436
  2.9 0.9 %copy-start.2 = (f32[1,1,64,8,128]{4,3,2,1,0:T(8,128)S(1)}, f32[1,1,64,8,128]{4,3,2,1,0:T(8,128)}, u32[]{:S(2)}) copy-start(f32[1,1,64,8,128]{4,3,2,1,0:T(8,128)} %param.6) | copy-start | bytes 786436
  3.8 0.7 %copy-start.3 = (f32[8,64]{1,0:T(8,128)S(1)}, f32[8,64]{1,0:T(8,128)}, u32[]{:S(2)}) copy-start(f32[8,64]{1,0:T(8,128)} %b_ref.1) | copy-start | bytes 6148
  4.5 0.7 %copy-start.4 = (f32[1,64]{1,0:T(1,128)S(1)}, f32[1,64]{1,0:T(1,128)}, u32[]{:S(2)}) copy-start(f32[1,64]{1,0:T(1,128)} %gain_ref.1) | copy-start | bytes 772

commit v3 on v2

--- a/solution.py
+++ b/solution.py
@@ -24,11 +24,11 @@
 
 
 def fused_kernel(
-    c_ref,
-    a_ref,
-    w_in,
-    b_ref,
-    gain_ref,
+    c_hbm,
+    a_hbm,
+    w_hbm,
+    b_hbm,
+    gain_hbm,
     pieces_out,
     grad_out,
     snd,
@@ -72,6 +72,12 @@
     gc_recv,
     gd_send,
     gd_recv,
+    c_ref,
+    a_ref,
+    w_in,
+    b_ref,
+    gain_ref,
+    load_sem,
 ):
     blocks = w_in.shape[0]
     layer = lax.axis_index("layer")
@@ -90,6 +96,21 @@
     own = jnp.where((lane >= HALO) & (lane < HALO + OWN), 1.0, 0.0).astype(F32)
     top = row == 0
 
+    loads = [
+        pltpu.make_async_copy(src, dst, load_sem.at[n])
+        for n, (src, dst) in enumerate(
+            (
+                (c_hbm, c_ref),
+                (a_hbm, a_ref),
+                (w_hbm, w_in),
+                (b_hbm, b_ref),
+                (gain_hbm, gain_ref),
+            )
+        )
+    ]
+    for load in loads:
+        load.start()
+
     barrier = pltpu.get_barrier_semaphore()
 
     def greet(n, carry):
@@ -158,10 +179,12 @@
                 {"row": 1 - row},
             ).wait_recv()
 
+    loads[0].wait()
     pack(c_ref, 0)
     pl.semaphore_wait(barrier, 2 * layers - 1 + 2 * (cols - 1))
     for copy in exchange(0):
         copy.start()
+    loads[1].wait()
     pack(a_ref, 1)
     for copy in exchange(1):
         copy.start()
@@ -175,6 +198,8 @@
             wt_ref[l, 64 * i : 64 * i + 64, :] = (0.5 * stack.astype(F32)).T.astype(BF)
         return carry
 
+    for load in loads[2:]:
+        load.wait()
     lax.fori_loop(0, blocks, lay_weights, 0)
     tmp[...] = jnp.zeros_like(tmp)
     tmp[0:blocks, 0:64] = 0.5 * b_ref[...]
@@ -188,6 +213,9 @@
     def holder(h):
         return 2 * lax.rem(h, 8) + row, h // 8
 
+    def turn(k):
+        return 8 * lax.rem(layer + k // 8, 2) + lax.rem(layer // 2 + k, 8)
+
     def stays(h):
         lam, rho = holder(h)
         return jnp.logical_and(lam == layer, rho == row)
@@ -215,7 +243,9 @@
     def comes(e):
         return jnp.logical_or(e != layer, lax.rem(layer, 2) != row)
 
-    def send_gain(h, carry):
+    def send_gain(k, carry):
+        h = turn(k)
+
         @pl.when(stays(h))
         def _():
             gain_rcv[layer] = gain_snd[...]
@@ -302,7 +332,8 @@
         gain = gain_own[...] * keep
         shift = jnp.where(top, 32, 96)
 
-        def one(h, carry):
+        def one(k, carry):
+            h = turn(k)
             rho, u = h // 8, lax.rem(h, 8)
             mine = pltpu.roll(guess_own[pl.ds(u, 64, stride=8), :], shift, 1)
             other = pltpu.roll(rcv[n, u].astype(F32), shift, 1)
@@ -336,9 +367,7 @@
         first = 0 if n == 0 else layers - 1
         stride = 1 if n == 0 else -1
 
-        def one(k, state):
-            e = first + stride * k
-
+        def take(e, carry):
             @pl.when(comes(e))
             def _():
                 remote(
@@ -349,32 +378,30 @@
                     {"layer": layer, "row": 1 - row},
                 ).wait_recv()
 
+            return carry
+
+        lax.fori_loop(0, layers, take, 0)
+        state = jnp.zeros((32, 128), F32)
+        for k in range(15):
+            e = first + stride * k
             state = gain_pk[e] * state + p1_rcv[n, e].astype(F32)
-            target = e + stride
-
-            @pl.when(target == layer)
+            p2_snd[n, e + stride] = state.astype(BF)
+        skipped = 0 if n == 0 else layers - 1
+
+        def give(k, carry):
+            e = lax.rem(layer + k, layers)
+
+            @pl.when(e != skipped)
             def _():
-                p2_rcv[n, layer] = state.astype(BF)
-
-            @pl.when(target != layer)
-            def _():
-                p2_snd[n, target] = state.astype(BF)
-                p2_copy(n, target).start()
-
-            return state
-
-        lax.fori_loop(0, layers - 1, one, jnp.zeros((32, 128), F32))
-        unused = layers - 1 if n == 0 else 0
-
-        @pl.when(comes(unused))
-        def _():
-            remote(
-                p1_snd.at[n, 0],
-                p1_rcv.at[n, unused],
-                p1_send.at[n, 0],
-                p1_recv.at[n, unused],
-                {"layer": layer, "row": 1 - row},
-            ).wait_recv()
+                p2_copy(n, e).start()
+
+            return carry
+
+        lax.fori_loop(1, layers, give, 0)
+
+        @pl.when(layer != skipped)
+        def _():
+            p2_rcv[n, layer] = p2_snd[n, layer]
 
     send_pieces(0, phi_ref, c_ref, jnp.where(layer == 0, 0.0, 1.0))
 
@@ -620,7 +647,7 @@
             jax.ShapeDtypeStruct((2, 16, 32, 128), BF),
             jax.ShapeDtypeStruct((blocks, 288, 128), BF),
         ),
-        in_specs=[pl.BlockSpec(memory_space=vm)] * 5,
+        in_specs=[pl.BlockSpec(memory_space=pltpu.HBM)] * 5,
         out_specs=[pl.BlockSpec(memory_space=vm)] * 2,
         scratch_shapes=[
             vm((2, 8, 64, 128), BF),
@@ -664,6 +691,12 @@
             dma((blocks,)),
             dma((blocks,)),
             dma((blocks,)),
+            vm(c.shape, F32),
+            vm(a.shape, F32),
+            vm(w.shape, BF),
+            vm(b.shape, F32),
+            vm(gain.shape, F32),
+            dma((5,)),
         ],
         compiler_params=pltpu.CompilerParams(
             vmem_limit_bytes=48 << 20, collective_id=0, has_side_effects=True
@@ -671,58 +704,69 @@
     )(c, a, w, b, gain)
 
 
-def unpack_kernel(c_ref, a_ref, pieces_ref, grad_ref, c_out, a_out, g_out):
+def unpack_kernel(c_ref, a_ref, pieces_ref, grad_ref, c_out, a_out, g_out, c_s, a_s, g_s, sem):
     layer = lax.axis_index("layer")
     layers = lax.axis_size("layer")
+    blocks = grad_ref.shape[0]
     lane32 = lax.broadcasted_iota(jnp.int32, (32, 128), 1)
 
-    @pl.when(pl.program_id(0) == 0)
-    def _():
-        for n, src, dst, skipped in ((0, c_ref, c_out, 0), (1, a_ref, a_out, layers - 1)):
-
-            @pl.when(layer == skipped)
-            def _():
-                dst[...] = src[...]
-
-            @pl.when(layer != skipped)
-            def _():
-                for u in range(8):
-                    left = pieces_ref[n, 2 * u].astype(F32)
-                    right = pieces_ref[n, 2 * u + 1].astype(F32)
-                    dst[pl.ds(u, 32, stride=8), :] = jnp.where(
-                        lane32 < 64, left, pltpu.roll(right, 64, 1)
-                    )
-                    dst[pl.ds(256 + u, 32, stride=8), :] = jnp.where(
-                        lane32 < 64, pltpu.roll(left, 64, 1), right
-                    )
-
-    for j in range(3):
-        g_out[0, j] = grad_ref[0, 64 * j : 64 * j + 64, 0:64].astype(F32)
-        g_out[0, 3 + j] = grad_ref[0, 64 * j : 64 * j + 64, 64:128].astype(F32)
-    g_out[0, 6] = grad_ref[0, 192:256, 0:64].astype(F32)
-    g_out[0, 7, 0:32] = grad_ref[0, 256:288, 0:64].astype(F32)
-    g_out[0, 7, 32:64] = grad_ref[0, 192:224, 64:128].astype(F32)
-    g_out[0, 8] = grad_ref[0, 224:288, 64:128].astype(F32)
+    def states(n, whole, part, out, skipped):
+        @pl.when(layer == skipped)
+        def _():
+            pltpu.make_async_copy(whole, out, sem.at[blocks + n]).start()
+
+        @pl.when(layer != skipped)
+        def _():
+            for u in range(8):
+                left = pieces_ref[n, 2 * u].astype(F32)
+                right = pieces_ref[n, 2 * u + 1].astype(F32)
+                part[pl.ds(u, 32, stride=8), :] = jnp.where(
+                    lane32 < 64, left, pltpu.roll(right, 64, 1)
+                )
+                part[pl.ds(256 + u, 32, stride=8), :] = jnp.where(
+                    lane32 < 64, pltpu.roll(left, 64, 1), right
+                )
+            pltpu.make_async_copy(part, out, sem.at[blocks + n]).start()
+
+    def one(l, carry):
+        for j in range(3):
+            g_s[l, j] = grad_ref[l, 64 * j : 64 * j + 64, 0:64].astype(F32)
+            g_s[l, 3 + j] = grad_ref[l, 64 * j : 64 * j + 64, 64:128].astype(F32)
+        g_s[l, 6] = grad_ref[l, 192:256, 0:64].astype(F32)
+        g_s[l, 7, 0:32] = grad_ref[l, 256:288, 0:64].astype(F32)
+        g_s[l, 7, 32:64] = grad_ref[l, 192:224, 64:128].astype(F32)
+        g_s[l, 8] = grad_ref[l, 224:288, 64:128].astype(F32)
+        pltpu.make_async_copy(g_s.at[l], g_out.at[l], sem.at[l]).start()
+        return carry
+
+    lax.fori_loop(0, blocks, one, 0)
+    states(0, c_ref, c_s, c_out, 0)
+    states(1, a_ref, a_s, a_out, layers - 1)
+    for l in range(blocks):
+        pltpu.make_async_copy(g_s.at[l], g_out.at[l], sem.at[l]).wait()
+    pltpu.make_async_copy(c_s, c_out, sem.at[blocks]).wait()
+    pltpu.make_async_copy(a_s, a_out, sem.at[blocks + 1]).wait()
 
 
 def unpack(c, a, pieces, grad):
     blocks = grad.shape[0]
-    whole = pl.BlockSpec((512, 128), lambda l: (0, 0))
+    vm = pltpu.VMEM
+    far = pl.BlockSpec(memory_space=pltpu.HBM)
     return pl.pallas_call(
         unpack_kernel,
-        grid=(blocks,),
         out_shape=(
             jax.ShapeDtypeStruct((512, 128), F32),
             jax.ShapeDtypeStruct((512, 128), F32),
             jax.ShapeDtypeStruct((blocks, 9, 64, 64), F32),
         ),
-        in_specs=[
-            whole,
-            whole,
-            pl.BlockSpec((2, 16, 32, 128), lambda l: (0, 0, 0, 0)),
-            pl.BlockSpec((1, 288, 128), lambda l: (l, 0, 0)),
+        in_specs=[far, far, pl.BlockSpec(memory_space=vm), pl.BlockSpec(memory_space=vm)],
+        out_specs=[far] * 3,
+        scratch_shapes=[
+            vm((512, 128), F32),
+            vm((512, 128), F32),
+            vm((blocks, 9, 64, 64), F32),
+            pltpu.SemaphoreType.DMA((blocks + 2,)),
         ],
-        out_specs=[whole, whole, pl.BlockSpec((1, 9, 64, 64), lambda l: (l, 0, 0, 0))],
         compiler_params=pltpu.CompilerParams(vmem_limit_bytes=32 << 20),
     )(c, a, pieces, grad)
 
@@ -730,8 +774,12 @@
 def local(c_guess, adjoint_guess, weights, biases, coarse_gain):
     c = c_guess.reshape(512, 128)
     a = adjoint_guess.reshape(512, 128)
-    pieces, grad = fused(c, a, weights, biases, coarse_gain)
-    c_states, ends, weight_grad = unpack(c, a, pieces, grad)
+    far = [
+        pltpu.with_memory_space_constraint(x, pltpu.HBM)
+        for x in (c, a, weights, biases, coarse_gain)
+    ]
+    pieces, grad = fused(*far)
+    c_states, ends, weight_grad = unpack(far[0], far[1], pieces, grad)
     return (c_states.reshape(c_guess.shape), ends.reshape(c_guess.shape), weight_grad)
 
 

time: 55.5 us -> 57.7 us (1.040)
  Pallas kernels: 50.1 us -> 56.9 us
  local copies, waits for them, and re-layouts: 4.5 us -> 0 us
    pallas_call x1, Pallas kernels: 3.67 us -> 9.86 us  [unpack(): pl.pallas_call(unpack_kernel, out_shape=(jax.ShapeDtypeStruct((512, 128),...]
    unnamed x10 -> x0, local copies, waits for them, and re-layouts: 4.5 us -> none
    pallas_call x1, Pallas kernels: 46.4 us -> 47 us  [fused(): pl.pallas_call(fused_kernel, out_shape=(jax.ShapeDtypeStruct((2, 16, 32,...]
where the time goes in v3:
time: 57.7 us; the launch traced here: 57.5 us
  Pallas kernels  56.9 us (99%)
  between operations  0.64 us (1%)
    pallas_call x1, Pallas kernels, fused(): pl.pallas_call(fused_kernel, out_shape=(jax.ShapeDtypeStruct((2, 16, 32,...  47 us
    pallas_call x1, Pallas kernels, unpack(): pl.pallas_call(unpack_kernel, out_shape=(jax.ShapeDtypeStruct((512, 128),...  9.86 us

profile of v3, /device:TPU:1, one launch (start us, length us, event | category | flops | bytes accessed | tf_op | source)
XLA Modules:
  0.0 57.5 jit_solution(15536298793010503269)
XLA Ops:
  0.6 47.0 %shard_map.76 = (bf16[2,16,32,128]{3,2,1,0:T(8,128)(2,1)S(1)}, bf16[8,288,128]{2,1,0:T(8,128)(2,1)S(1)}) custom-call(f32[512,128]{1,0:T(8,128)} %bitcast.4, f32[512,128]{1,0:T(8,128)} %bitcast.6, bf16[8,9,64,64]{3,2,1,0:T(8,128)(2,1)} %w_hbm.1, f32[8,64]{1,0:T(8,128)} %b_hbm.1, f32[1,64]{1,0:T(1,128)} %gain_hbm.1), custom_call_target="tpu_custom_call" | custom-call | tf_op jit(solution)/shard_map/pallas_call | solution.py:644
  47.7 9.9 %shard_map.77 = (f32[512,128]{1,0:T(8,128)}, f32[512,128]{1,0:T(8,128)}, f32[8,9,64,64]{3,2,1,0:T(8,128)}) custom-call(f32[512,128]{1,0:T(8,128)} %bitcast.5, f32[512,128]{1,0:T(8,128)} %bitcast.7, bf16[2,16,32,128]{3,2,1,0:T(8,128)(2,1)S(1)} %get-tuple-element.8.pieces_ref, bf16[8,288,128]{2,1,0:T(8,128)(2,1)S(1)} %get-tuple-element.9.grad_ref), custom_call_target="tpu_custom_call" | custom-call | tf_op jit(solution)/shard_map/pallas_call | solution.py:755

commit v4 on v3

--- a/solution.py
+++ b/solution.py
@@ -78,6 +78,7 @@
     b_ref,
     gain_ref,
     load_sem,
+    q_s,
 ):
     blocks = w_in.shape[0]
     layer = lax.axis_index("layer")
@@ -113,24 +114,21 @@
 
     barrier = pltpu.get_barrier_semaphore()
 
-    def greet(n, carry):
-        e, rho = n // 2, lax.rem(n, 2)
-
-        @pl.when(jnp.logical_or(e != layer, rho != row))
-        def _():
-            pl.semaphore_signal(
-                barrier, inc=1, device_id={"layer": e, "row": rho}, device_id_type=MESH
-            )
-
-        return carry
-
-    lax.fori_loop(0, 2 * layers, greet, 0)
+    pl.semaphore_signal(barrier, inc=1, device_id={"row": 1 - row}, device_id_type=MESH)
     for step in range(1, cols):
         for rho in range(2):
             pl.semaphore_signal(
                 barrier,
                 inc=1,
                 device_id={"row": rho, "col": lax.rem(col + step, cols)},
+                device_id_type=MESH,
+            )
+    for step in range(1, layers):
+        for rho in range(2):
+            pl.semaphore_signal(
+                barrier,
+                inc=1,
+                device_id={"layer": lax.rem(layer + step, layers), "row": rho},
                 device_id_type=MESH,
             )
 
@@ -331,28 +329,30 @@
     def send_pieces(n, field, guess_own, keep):
         gain = gain_own[...] * keep
         shift = jnp.where(top, 32, 96)
+        for u in range(8):
+            for rho, guess in (
+                (row, guess_own[pl.ds(u, 64, stride=8), :]),
+                (1 - row, rcv[n, u].astype(F32)),
+            ):
+                r = field[8 * rho + u] - gain * pltpu.roll(guess, shift, 1)
+                p1_snd[n, 8 * rho + u] = jnp.where(
+                    lane32 < 64, pltpu.roll(r[:32], 96, 1), pltpu.roll(r[32:], 32, 1)
+                ).astype(BF)
 
         def one(k, carry):
             h = turn(k)
-            rho, u = h // 8, lax.rem(h, 8)
-            mine = pltpu.roll(guess_own[pl.ds(u, 64, stride=8), :], shift, 1)
-            other = pltpu.roll(rcv[n, u].astype(F32), shift, 1)
-            here = jnp.where(rho == row, 1.0, 0.0)
-            r = field[h] - gain * (here * mine + (1.0 - here) * other)
-            packed = jnp.where(lane32 < 64, pltpu.roll(r[:32], 96, 1), pltpu.roll(r[32:], 32, 1))
-
-            @pl.when(stays(h))
-            def _():
-                p1_rcv[n, layer] = packed.astype(BF)
 
             @pl.when(jnp.logical_not(stays(h)))
             def _():
-                p1_snd[n, h] = packed.astype(BF)
                 p1_copy(n, h).start()
 
             return carry
 
         lax.fori_loop(0, 16, one, 0)
+
+        @pl.when(lax.rem(layer, 2) == row)
+        def _():
+            p1_rcv[n, layer] = p1_snd[n, 8 * row + layer // 2]
 
     def p2_copy(n, e):
         return remote(
@@ -498,11 +498,9 @@
     def backward(step, carry):
         l = blocks - 1 - step
         wt = wt_ref[l]
-        grad = jnp.zeros((192, 192), F32)
         later, last = None, None
         for m in range(8):
             pieces = []
-            zs = []
             for h in (2 * m, 2 * m + 1):
                 a = psi_ref[h]
                 pieces.append(
@@ -515,13 +513,9 @@
                         axis=0,
                     )
                 )
-                zs.append(jnp.concatenate([z_s[l, h], z_s[l, h + 1], z_s[l, h + 2]], axis=0))
             rhs = jnp.concatenate(pieces, axis=1)
-            zz = jnp.concatenate(zs, axis=1)
+            q_s[l, m] = rhs
             prod = jnp.dot(wt, rhs, preferred_element_type=F32)
-            grad = grad + lax.dot_general(
-                rhs, zz, (((1,), (1,)), ((), ())), preferred_element_type=F32
-            )
             p0, p1 = prod[:, :128], prod[:, 128:]
             if m > 0:
                 psi_ref[2 * m - 1] = psi_ref[2 * m - 1] + sl_s[l, 2 * m - 1] * (later + p0[:64])
@@ -532,28 +526,42 @@
             later = p0[128:] + p1[64:128]
             last = p1[128:]
         psi_ref[15] = psi_ref[15] + sl_s[l, 15] * later
+        return carry
+
+    lax.fori_loop(0, blocks, backward, 0)
+    send_pieces(1, psi_ref, a_ref, jnp.where(layer == layers - 1, 0.0, 1.0))
+
+    def weight_grads(step, carry):
+        l = blocks - 1 - step
+        grad = jnp.zeros((192, 192), F32)
+        for m in range(8):
+            zz = jnp.concatenate(
+                [
+                    jnp.concatenate([z_s[l, h], z_s[l, h + 1], z_s[l, h + 2]], axis=0)
+                    for h in (2 * m, 2 * m + 1)
+                ],
+                axis=1,
+            )
+            grad = grad + lax.dot_general(
+                q_s[l, m], zz, (((1,), (1,)), ((), ())), preferred_element_type=F32
+            )
         grad = 0.5 * grad
         g_part[l, 0:192, :] = grad[:, :128]
         g_part[l, 192:288, 0:64] = grad[:96, 128:192]
         g_part[l, 192:288, 64:128] = grad[96:, 128:192]
         ga_copy(l).start()
 
-        @pl.when(step >= 2)
-        def _():
-            to_owner(l + 2)
-
-        @pl.when(step == 5)
-        def _():
-            solve(0)
-
-        return carry
-
-    lax.fori_loop(0, blocks, backward, 0)
-
-    send_pieces(1, psi_ref, a_ref, jnp.where(layer == layers - 1, 0.0, 1.0))
+        @pl.when(step >= 3)
+        def _():
+            to_owner(l + 3)
+
+        return carry
+
+    lax.fori_loop(0, blocks, weight_grads, 0)
+    for l in (2, 1, 0):
+        to_owner(l)
+    solve(0)
     own_block(1)
-    to_owner(1)
-    to_owner(0)
     solve(1)
     own_block(0)
 
@@ -697,6 +705,7 @@
             vm(b.shape, F32),
             vm(gain.shape, F32),
             dma((5,)),
+            vm((blocks, 8, 192, 256), BF),
         ],
         compiler_params=pltpu.CompilerParams(
             vmem_limit_bytes=48 << 20, collective_id=0, has_side_effects=True
@@ -710,10 +719,16 @@
     blocks = grad_ref.shape[0]
     lane32 = lax.broadcasted_iota(jnp.int32, (32, 128), 1)
 
+    for n, whole, part, skipped in ((0, c_ref, c_s, 0), (1, a_ref, a_s, layers - 1)):
+
+        @pl.when(layer == skipped)
+        def _():
+            pltpu.make_async_copy(whole, part, sem.at[blocks + 2 + n]).start()
+
     def states(n, whole, part, out, skipped):
         @pl.when(layer == skipped)
         def _():
-            pltpu.make_async_copy(whole, out, sem.at[blocks + n]).start()
+            pltpu.make_async_copy(whole, part, sem.at[blocks + 2 + n]).wait()
 
         @pl.when(layer != skipped)
         def _():
@@ -726,7 +741,7 @@
                 part[pl.ds(256 + u, 32, stride=8), :] = jnp.where(
                     lane32 < 64, pltpu.roll(left, 64, 1), right
                 )
-            pltpu.make_async_copy(part, out, sem.at[blocks + n]).start()
+        pltpu.make_async_copy(part, out, sem.at[blocks + n]).start()
 
     def one(l, carry):
         for j in range(3):
@@ -765,7 +780,7 @@
             vm((512, 128), F32),
             vm((512, 128), F32),
             vm((blocks, 9, 64, 64), F32),
-            pltpu.SemaphoreType.DMA((blocks + 2,)),
+            pltpu.SemaphoreType.DMA((blocks + 4,)),
         ],
         compiler_params=pltpu.CompilerParams(vmem_limit_bytes=32 << 20),
     )(c, a, pieces, grad)

time: 57.7 us -> 47.4 us (0.82)
  Pallas kernels: 56.9 us -> 46.6 us
    pallas_call x1, Pallas kernels: 9.86 us -> 1.89 us  [unpack(): pl.pallas_call(unpack_kernel, out_shape=(jax.ShapeDtypeStruct((512, 128),...]
    pallas_call x1, Pallas kernels: 47 us -> 44.7 us  [fused(): pl.pallas_call(fused_kernel, out_shape=(jax.ShapeDtypeStruct((2, 16, 32,...]
where the time goes in v4:
time: 47.4 us; the launch traced here: 47.3 us
  Pallas kernels  46.6 us (98%)
  between operations  0.64 us (1%)
    pallas_call x1, Pallas kernels, fused(): pl.pallas_call(fused_kernel, out_shape=(jax.ShapeDtypeStruct((2, 16, 32,...  44.7 us
    pallas_call x1, Pallas kernels, unpack(): pl.pallas_call(unpack_kernel, out_shape=(jax.ShapeDtypeStruct((512, 128),...  1.89 us

profile of v4, /device:TPU:1, one launch (start us, length us, event | category | flops | bytes accessed | tf_op | source)
XLA Modules:
  0.0 47.3 jit_solution(1752521056596911829)
XLA Ops:
  0.6 44.7 %shard_map.76 = (bf16[2,16,32,128]{3,2,1,0:T(8,128)(2,1)S(1)}, bf16[8,288,128]{2,1,0:T(8,128)(2,1)S(1)}) custom-call(f32[512,128]{1,0:T(8,128)} %bitcast.4, f32[512,128]{1,0:T(8,128)} %bitcast.6, bf16[8,9,64,64]{3,2,1,0:T(8,128)(2,1)} %w_hbm.1, f32[8,64]{1,0:T(8,128)} %b_hbm.1, f32[1,64]{1,0:T(1,128)} %gain_hbm.1), custom_call_target="tpu_custom_call" | custom-call | tf_op jit(solution)/shard_map/pallas_call | solution.py:652
  45.4 1.9 %shard_map.77 = (f32[512,128]{1,0:T(8,128)}, f32[512,128]{1,0:T(8,128)}, f32[8,9,64,64]{3,2,1,0:T(8,128)}) custom-call(f32[512,128]{1,0:T(8,128)} %bitcast.5, f32[512,128]{1,0:T(8,128)} %bitcast.7, bf16[2,16,32,128]{3,2,1,0:T(8,128)(2,1)S(1)} %get-tuple-element.8.pieces_ref, bf16[8,288,128]{2,1,0:T(8,128)(2,1)S(1)} %get-tuple-element.9.grad_ref), custom_call_target="tpu_custom_call" | custom-call | tf_op jit(solution)/shard_map/pallas_call | solution.py:770

commit v5 on v4

--- a/solution.py
+++ b/solution.py
@@ -211,8 +211,23 @@
     def holder(h):
         return 2 * lax.rem(h, 8) + row, h // 8
 
-    def turn(k):
-        return 8 * lax.rem(layer + k // 8, 2) + lax.rem(layer // 2 + k, 8)
+    rows_far_first = [
+        8 * rho + lax.rem(layer // 2 + k, 8) for rho in (1 - row, row) for k in (5, 3, 4, 6, 2, 7, 1, 0)
+    ]
+    layers_far_first = [
+        4 * lax.rem(layer // 4 + dx, 4) + lax.rem(layer + dz, 4)
+        for dx, dz in (
+            (2, 2), (2, 1), (2, 3), (1, 2), (3, 2), (1, 1), (3, 3), (1, 3), (3, 1),
+            (2, 0), (0, 2), (1, 0), (3, 0), (0, 1), (0, 3),
+        )
+    ]
+
+    def all_but_own(count, wait):
+        for own_piece in (True, False):
+
+            @pl.when((lax.rem(layer, 2) == row) == own_piece)
+            def _():
+                wait(count - 1 if own_piece else count)
 
     def stays(h):
         lam, rho = holder(h)
@@ -223,8 +238,8 @@
         return remote(
             gain_snd,
             gain_rcv.at[layer],
-            gain_send.at[h],
-            gain_recv.at[layer],
+            gain_send.at[0],
+            gain_recv.at[0],
             {"layer": lam, "row": rho},
         )
 
@@ -233,28 +248,22 @@
         return remote(
             p1_snd.at[n, h],
             p1_rcv.at[n, layer],
-            p1_send.at[n, h],
-            p1_recv.at[n, layer],
+            p1_send.at[n],
+            p1_recv.at[n],
             {"layer": lam, "row": rho},
         )
 
-    def comes(e):
-        return jnp.logical_or(e != layer, lax.rem(layer, 2) != row)
-
-    def send_gain(k, carry):
-        h = turn(k)
-
-        @pl.when(stays(h))
-        def _():
-            gain_rcv[layer] = gain_snd[...]
-
+    def start_unless_here(h, copy):
         @pl.when(jnp.logical_not(stays(h)))
         def _():
-            gain_copy(h).start()
-
-        return carry
-
-    lax.fori_loop(0, 16, send_gain, 0)
+            copy.start()
+
+    for h in rows_far_first:
+        start_unless_here(h, gain_copy(h))
+
+    @pl.when(lax.rem(layer, 2) == row)
+    def _():
+        gain_rcv[layer] = gain_snd[...]
 
     def assemble(src, n, dst):
         shift = jnp.where(top, 32, 96)
@@ -339,16 +348,8 @@
                     lane32 < 64, pltpu.roll(r[:32], 96, 1), pltpu.roll(r[32:], 32, 1)
                 ).astype(BF)
 
-        def one(k, carry):
-            h = turn(k)
-
-            @pl.when(jnp.logical_not(stays(h)))
-            def _():
-                p1_copy(n, h).start()
-
-            return carry
-
-        lax.fori_loop(0, 16, one, 0)
+        for h in rows_far_first:
+            start_unless_here(h, p1_copy(n, h))
 
         @pl.when(lax.rem(layer, 2) == row)
         def _():
@@ -358,8 +359,8 @@
         return remote(
             p2_snd.at[n, e],
             p2_rcv.at[n, layer],
-            p2_send.at[n, e],
-            p2_recv.at[n, layer],
+            p2_send.at[n],
+            p2_recv.at[n],
             {"layer": e},
         )
 
@@ -367,20 +368,16 @@
         first = 0 if n == 0 else layers - 1
         stride = 1 if n == 0 else -1
 
-        def take(e, carry):
-            @pl.when(comes(e))
-            def _():
-                remote(
-                    p1_snd.at[n, 0],
-                    p1_rcv.at[n, e],
-                    p1_send.at[n, 0],
-                    p1_recv.at[n, e],
-                    {"layer": layer, "row": 1 - row},
-                ).wait_recv()
-
-            return carry
-
-        lax.fori_loop(0, layers, take, 0)
+        all_but_own(
+            16,
+            lambda count: remote(
+                p1_snd.at[n, pl.ds(0, count)],
+                p1_rcv.at[n, pl.ds(0, count)],
+                p1_send.at[n],
+                p1_recv.at[n],
+                {"row": 1 - row},
+            ).wait_recv(),
+        )
         state = jnp.zeros((32, 128), F32)
         for k in range(15):
             e = first + stride * k
@@ -388,37 +385,28 @@
             p2_snd[n, e + stride] = state.astype(BF)
         skipped = 0 if n == 0 else layers - 1
 
-        def give(k, carry):
-            e = lax.rem(layer + k, layers)
+        for e in layers_far_first:
 
             @pl.when(e != skipped)
             def _():
                 p2_copy(n, e).start()
 
-            return carry
-
-        lax.fori_loop(1, layers, give, 0)
-
         @pl.when(layer != skipped)
         def _():
             p2_rcv[n, layer] = p2_snd[n, layer]
 
     send_pieces(0, phi_ref, c_ref, jnp.where(layer == 0, 0.0, 1.0))
 
-    def take_gain(e, carry):
-        @pl.when(comes(e))
-        def _():
-            remote(
-                gain_snd,
-                gain_rcv.at[e],
-                gain_send.at[0],
-                gain_recv.at[e],
-                {"layer": layer, "row": 1 - row},
-            ).wait_recv()
-
-        return carry
-
-    lax.fori_loop(0, layers, take_gain, 0)
+    all_but_own(
+        16,
+        lambda count: remote(
+            gain_rcv.at[pl.ds(0, count)],
+            gain_rcv.at[pl.ds(0, count)],
+            gain_send.at[0],
+            gain_recv.at[0],
+            {"row": 1 - row},
+        ).wait_recv(),
+    )
     for e in range(16):
         tmp[e : e + 1, :] = gain_rcv[e, 0:1, :]
     turned_all = tmp[...].T
@@ -514,7 +502,7 @@
                     )
                 )
             rhs = jnp.concatenate(pieces, axis=1)
-            q_s[l, m] = rhs
+            q_s[l, :, 256 * m : 256 * m + 256] = rhs
             prod = jnp.dot(wt, rhs, preferred_element_type=F32)
             p0, p1 = prod[:, :128], prod[:, 128:]
             if m > 0:
@@ -533,18 +521,16 @@
 
     def weight_grads(step, carry):
         l = blocks - 1 - step
-        grad = jnp.zeros((192, 192), F32)
-        for m in range(8):
-            zz = jnp.concatenate(
-                [
-                    jnp.concatenate([z_s[l, h], z_s[l, h + 1], z_s[l, h + 2]], axis=0)
-                    for h in (2 * m, 2 * m + 1)
-                ],
-                axis=1,
-            )
-            grad = grad + lax.dot_general(
-                q_s[l, m], zz, (((1,), (1,)), ((), ())), preferred_element_type=F32
-            )
+        zz = jnp.concatenate(
+            [
+                jnp.concatenate([z_s[l, h], z_s[l, h + 1], z_s[l, h + 2]], axis=0)
+                for h in range(16)
+            ],
+            axis=1,
+        )
+        grad = lax.dot_general(
+            q_s[l], zz, (((1,), (1,)), ((), ())), preferred_element_type=F32
+        )
         grad = 0.5 * grad
         g_part[l, 0:192, :] = grad[:, :128]
         g_part[l, 192:288, 0:64] = grad[:96, 128:192]
@@ -555,14 +541,17 @@
         def _():
             to_owner(l + 3)
 
+        @pl.when(step == 5)
+        def _():
+            solve(0)
+
         return carry
 
     lax.fori_loop(0, blocks, weight_grads, 0)
     for l in (2, 1, 0):
         to_owner(l)
-    solve(0)
+    solve(1)
     own_block(1)
-    solve(1)
     own_block(0)
 
     def forward_half(k, carry):
@@ -587,33 +576,46 @@
         for copy in exchange(n):
             copy.wait_send()
 
-    def drain(h, carry):
-        @pl.when(jnp.logical_not(stays(h)))
-        def _():
-            gain_copy(h).wait_send()
-            for n in range(2):
-                p1_copy(n, h).wait_send()
-
+    def sent(count):
+        remote(
+            gain_rcv.at[pl.ds(0, count)],
+            gain_rcv.at[pl.ds(0, count)],
+            gain_send.at[0],
+            gain_recv.at[0],
+            {"row": 1 - row},
+        ).wait_send()
         for n in range(2):
-            skipped = 0 if n == 0 else layers - 1
-
-            @pl.when(jnp.logical_and(h != layer, h != skipped))
-            def _():
-                p2_copy(n, h).wait_send()
-
-            @pl.when(jnp.logical_and(h != layer, layer != skipped))
-            def _():
-                remote(
-                    p2_snd.at[n, 0],
-                    p2_rcv.at[n, h],
-                    p2_send.at[n, 0],
-                    p2_recv.at[n, h],
-                    {"row": 1 - row},
-                ).wait_recv()
-
-        return carry
-
-    lax.fori_loop(0, 16, drain, 0)
+            remote(
+                p1_snd.at[n, pl.ds(0, count)],
+                p1_rcv.at[n, pl.ds(0, count)],
+                p1_send.at[n],
+                p1_recv.at[n],
+                {"row": 1 - row},
+            ).wait_send()
+
+    all_but_own(16, sent)
+
+    def p2_bytes(n, count):
+        return remote(
+            p2_snd.at[n, pl.ds(0, count)],
+            p2_rcv.at[n, pl.ds(0, count)],
+            p2_send.at[n],
+            p2_recv.at[n],
+            {"row": 1 - row},
+        )
+
+    for n in range(2):
+        skipped = 0 if n == 0 else layers - 1
+
+        @pl.when(layer == skipped)
+        def _():
+            p2_bytes(n, 15).wait_send()
+
+        @pl.when(layer != skipped)
+        def _():
+            p2_bytes(n, 14).wait_send()
+            p2_bytes(n, 15).wait_recv()
+            pieces_out[n] = p2_rcv[n]
 
     def drain_grads(l, carry):
         ga_copy(l).wait_send()
@@ -636,12 +638,6 @@
     for q in range(2):
         for step in range(1, 4):
             gc_copy(4 * q + chip, step).wait_send()
-    for n in range(2):
-
-        @pl.when(layer != (0 if n == 0 else layers - 1))
-        def _():
-            pieces_out[n] = p2_rcv[n]
-
     grad_out[...] = g_full[...]
 
 
@@ -685,12 +681,12 @@
             vm((blocks, 288, 128), BF),
             dma((2, 3)),
             dma((2, 3)),
-            dma((16,)),
-            dma((16,)),
-            dma((2, 16)),
-            dma((2, 16)),
-            dma((2, 16)),
-            dma((2, 16)),
+            dma((1,)),
+            dma((1,)),
+            dma((2,)),
+            dma((2,)),
+            dma((2,)),
+            dma((2,)),
             dma((blocks,)),
             dma((blocks,)),
             dma((blocks,)),
@@ -705,7 +701,7 @@
             vm(b.shape, F32),
             vm(gain.shape, F32),
             dma((5,)),
-            vm((blocks, 8, 192, 256), BF),
+            vm((blocks, 192, 2048), BF),
         ],
         compiler_params=pltpu.CompilerParams(
             vmem_limit_bytes=48 << 20, collective_id=0, has_side_effects=True

time: 47.4 us -> 44.7 us (0.943)
  Pallas kernels: 46.6 us -> 43.9 us
    pallas_call x1, Pallas kernels: 44.7 us -> 42 us  [fused(): pl.pallas_call(fused_kernel, out_shape=(jax.ShapeDtypeStruct((2, 16, 32,...]
where the time goes in v5:
time: 44.7 us; the launch traced here: 44.6 us
  Pallas kernels  43.9 us (98%)
  between operations  0.64 us (1%)
    pallas_call x1, Pallas kernels, fused(): pl.pallas_call(fused_kernel, out_shape=(jax.ShapeDtypeStruct((2, 16, 32,...  42 us
    pallas_call x1, Pallas kernels, unpack(): pl.pallas_call(unpack_kernel, out_shape=(jax.ShapeDtypeStruct((512, 128),...  1.89 us

profile of v5, /device:TPU:1, one launch (start us, length us, event | category | flops | bytes accessed | tf_op | source)
XLA Modules:
  0.0 44.6 jit_solution(3573131910299438813)
XLA Ops:
  0.6 42.0 %shard_map.76 = (bf16[2,16,32,128]{3,2,1,0:T(8,128)(2,1)S(1)}, bf16[8,288,128]{2,1,0:T(8,128)(2,1)S(1)}) custom-call(f32[512,128]{1,0:T(8,128)} %bitcast.4, f32[512,128]{1,0:T(8,128)} %bitcast.6, bf16[8,9,64,64]{3,2,1,0:T(8,128)(2,1)} %w_hbm.1, f32[8,64]{1,0:T(8,128)} %b_hbm.1, f32[1,64]{1,0:T(1,128)} %gain_hbm.1), custom_call_target="tpu_custom_call" | custom-call | tf_op jit(solution)/shard_map/pallas_call | solution.py:648
  42.7 1.9 %shard_map.77 = (f32[512,128]{1,0:T(8,128)}, f32[512,128]{1,0:T(8,128)}, f32[8,9,64,64]{3,2,1,0:T(8,128)}) custom-call(f32[512,128]{1,0:T(8,128)} %bitcast.5, f32[512,128]{1,0:T(8,128)} %bitcast.7, bf16[2,16,32,128]{3,2,1,0:T(8,128)(2,1)S(1)} %get-tuple-element.8.pieces_ref, bf16[8,288,128]{2,1,0:T(8,128)(2,1)S(1)} %get-tuple-element.9.grad_ref), custom_call_target="tpu_custom_call" | custom-call | tf_op jit(solution)/shard_map/pallas_call | solution.py:766

commit v6 on v5

--- a/solution.py
+++ b/solution.py
@@ -7,6 +7,7 @@
 
 HALO = 32
 OWN = 64
+SPLIT = 4
 BF = jnp.bfloat16
 F32 = jnp.float32
 MESH = pl.DeviceIdType.MESH
@@ -50,12 +51,10 @@
     p1_snd,
     p1_rcv,
     p2_snd,
-    p2_rcv,
     g_part,
     g_sib,
     g_half,
     g_chip,
-    g_full,
     in_send,
     in_recv,
     gain_send,
@@ -358,7 +357,7 @@
     def p2_copy(n, e):
         return remote(
             p2_snd.at[n, e],
-            p2_rcv.at[n, layer],
+            pieces_out.at[n, layer],
             p2_send.at[n],
             p2_recv.at[n],
             {"layer": e},
@@ -393,7 +392,7 @@
 
         @pl.when(layer != skipped)
         def _():
-            p2_rcv[n, layer] = p2_snd[n, layer]
+            pieces_out[n, layer] = p2_snd[n, layer]
 
     send_pieces(0, phi_ref, c_ref, jnp.where(layer == 0, 0.0, 1.0))
 
@@ -440,15 +439,15 @@
     def gc_copy(l, step):
         y = lax.rem(chip + step, 4)
         return remote(
-            g_full.at[l, half],
-            g_full.at[l, half],
+            grad_out.at[l, half],
+            grad_out.at[l, half],
             gc_send.at[l // 4, step - 1],
             gc_recv.at[l],
             at_chip(y),
         )
 
     def gd_copy(l):
-        return remote(g_full.at[l, half], g_full.at[l, half], gd_send.at[l], gd_recv.at[l], beside)
+        return remote(grad_out.at[l, half], grad_out.at[l, half], gd_send.at[l], gd_recv.at[l], beside)
 
     def to_owner(l):
         ga_copy(l).wait_recv()
@@ -476,15 +475,32 @@
             ).wait_recv()
         total = g_chip[q, 0].astype(F32) + g_chip[q, 1].astype(F32)
         total = total + g_chip[q, 2].astype(F32) + g_chip[q, 3].astype(F32)
-        g_full[l, half, :] = total.astype(BF)
+        grad_out[l, half, :] = total.astype(BF)
         for step in range(1, 4):
             gc_copy(l, step).start()
 
     arrived(1)
     assemble(a_ref, 1, psi_ref)
 
-    def backward(step, carry):
+    def keep_grad(l, grad):
+        grad = 0.5 * grad
+        g_part[l, 0:192, :] = grad[:, :128]
+        g_part[l, 192:288, 0:64] = grad[:96, 128:192]
+        g_part[l, 192:288, 64:128] = grad[96:, 128:192]
+        ga_copy(l).start()
+
+    def rows_of(l, first, last):
+        return jnp.concatenate(
+            [
+                jnp.concatenate([z_s[l, h], z_s[l, h + 1], z_s[l, h + 2]], axis=0)
+                for h in range(first, last)
+            ],
+            axis=1,
+        )
+
+    def backward(step, with_grad):
         l = blocks - 1 - step
+        grad = jnp.zeros((192, 192), F32)
         wt = wt_ref[l]
         later, last = None, None
         for m in range(8):
@@ -502,7 +518,15 @@
                     )
                 )
             rhs = jnp.concatenate(pieces, axis=1)
-            q_s[l, :, 256 * m : 256 * m + 256] = rhs
+            if with_grad:
+                grad = grad + lax.dot_general(
+                    rhs,
+                    rows_of(l, 2 * m, 2 * m + 2),
+                    (((1,), (1,)), ((), ())),
+                    preferred_element_type=F32,
+                )
+            else:
+                q_s[l, :, 256 * m : 256 * m + 256] = rhs
             prod = jnp.dot(wt, rhs, preferred_element_type=F32)
             p0, p1 = prod[:, :128], prod[:, 128:]
             if m > 0:
@@ -514,30 +538,36 @@
             later = p0[128:] + p1[64:128]
             last = p1[128:]
         psi_ref[15] = psi_ref[15] + sl_s[l, 15] * later
+        if with_grad:
+            keep_grad(l, grad)
+
+    def sweep_grads(step, carry):
+        backward(step, True)
+
+        @pl.when(step >= 2)
+        def _():
+            to_owner(blocks + 1 - step)
+
         return carry
 
-    lax.fori_loop(0, blocks, backward, 0)
+    def sweep(step, carry):
+        backward(step, False)
+        return carry
+
+    lax.fori_loop(0, SPLIT, sweep_grads, 0)
+    lax.fori_loop(SPLIT, blocks, sweep, 0)
     send_pieces(1, psi_ref, a_ref, jnp.where(layer == layers - 1, 0.0, 1.0))
 
     def weight_grads(step, carry):
         l = blocks - 1 - step
-        zz = jnp.concatenate(
-            [
-                jnp.concatenate([z_s[l, h], z_s[l, h + 1], z_s[l, h + 2]], axis=0)
-                for h in range(16)
-            ],
-            axis=1,
-        )
-        grad = lax.dot_general(
-            q_s[l], zz, (((1,), (1,)), ((), ())), preferred_element_type=F32
-        )
-        grad = 0.5 * grad
-        g_part[l, 0:192, :] = grad[:, :128]
-        g_part[l, 192:288, 0:64] = grad[:96, 128:192]
-        g_part[l, 192:288, 64:128] = grad[96:, 128:192]
-        ga_copy(l).start()
-
-        @pl.when(step >= 3)
+        keep_grad(
+            l,
+            lax.dot_general(
+                q_s[l], rows_of(l, 0, 16), (((1,), (1,)), ((), ())), preferred_element_type=F32
+            ),
+        )
+
+        @pl.when(step >= SPLIT + 1)
         def _():
             to_owner(l + 3)
 
@@ -547,7 +577,7 @@
 
         return carry
 
-    lax.fori_loop(0, blocks, weight_grads, 0)
+    lax.fori_loop(SPLIT, blocks, weight_grads, 0)
     for l in (2, 1, 0):
         to_owner(l)
     solve(1)
@@ -560,8 +590,8 @@
         @pl.when(lax.rem(l, 4) != chip)
         def _():
             remote(
-                g_full.at[l, half],
-                g_full.at[l, half],
+                grad_out.at[l, half],
+                grad_out.at[l, half],
                 gc_send.at[0, 0],
                 gc_recv.at[l],
                 at_chip(lax.rem(l, 4)),
@@ -598,7 +628,7 @@
     def p2_bytes(n, count):
         return remote(
             p2_snd.at[n, pl.ds(0, count)],
-            p2_rcv.at[n, pl.ds(0, count)],
+            pieces_out.at[n, pl.ds(0, count)],
             p2_send.at[n],
             p2_recv.at[n],
             {"row": 1 - row},
@@ -615,7 +645,6 @@
         def _():
             p2_bytes(n, 14).wait_send()
             p2_bytes(n, 15).wait_recv()
-            pieces_out[n] = p2_rcv[n]
 
     def drain_grads(l, carry):
         ga_copy(l).wait_send()
@@ -626,8 +655,8 @@
 
         gd_copy(l).wait_send()
         remote(
-            g_full.at[l, other_half],
-            g_full.at[l, other_half],
+            grad_out.at[l, other_half],
+            grad_out.at[l, other_half],
             gd_send.at[l],
             gd_recv.at[l],
             beside,
@@ -638,7 +667,6 @@
     for q in range(2):
         for step in range(1, 4):
             gc_copy(4 * q + chip, step).wait_send()
-    grad_out[...] = g_full[...]
 
 
 def fused(c, a, w, b, gain):
@@ -673,12 +701,10 @@
             vm((2, 16, 32, 128), BF),
             vm((2, 16, 32, 128), BF),
             vm((2, 16, 32, 128), BF),
-            vm((2, 16, 32, 128), BF),
             vm((blocks, 288, 128), F32),
             vm((blocks, 144, 128), F32),
             vm((blocks, 144, 128), BF),
             vm((2, 4, 144, 128), BF),
-            vm((blocks, 288, 128), BF),
             dma((2, 3)),
             dma((2, 3)),
             dma((1,)),

time: 44.7 us -> 43.7 us (0.978)
  Pallas kernels: 43.9 us -> 42.9 us
    pallas_call x1, Pallas kernels: 42 us -> 41.1 us  [fused(): pl.pallas_call(fused_kernel, out_shape=(jax.ShapeDtypeStruct((2, 16, 32,...]
where the time goes in v6:
time: 43.7 us; the launch traced here: 43.6 us
  Pallas kernels  42.9 us (98%)
  between operations  0.64 us (1%)
    pallas_call x1, Pallas kernels, fused(): pl.pallas_call(fused_kernel, out_shape=(jax.ShapeDtypeStruct((2, 16, 32,...  41.1 us
    pallas_call x1, Pallas kernels, unpack(): pl.pallas_call(unpack_kernel, out_shape=(jax.ShapeDtypeStruct((512, 128),...  1.89 us

profile of v6, /device:TPU:1, one launch (start us, length us, event | category | flops | bytes accessed | tf_op | source)
XLA Modules:
  0.0 43.6 jit_solution(15527184388199381686)
XLA Ops:
  0.6 41.1 %shard_map.76 = (bf16[2,16,32,128]{3,2,1,0:T(8,128)(2,1)S(1)}, bf16[8,288,128]{2,1,0:T(8,128)(2,1)S(1)}) custom-call(f32[512,128]{1,0:T(8,128)} %bitcast.4, f32[512,128]{1,0:T(8,128)} %bitcast.6, bf16[8,9,64,64]{3,2,1,0:T(8,128)(2,1)} %w_hbm.1, f32[8,64]{1,0:T(8,128)} %b_hbm.1, f32[1,64]{1,0:T(1,128)} %gain_hbm.1), custom_call_target="tpu_custom_call" | custom-call | tf_op jit(solution)/shard_map/pallas_call | solution.py:676
  41.7 1.9 %shard_map.77 = (f32[512,128]{1,0:T(8,128)}, f32[512,128]{1,0:T(8,128)}, f32[8,9,64,64]{3,2,1,0:T(8,128)}) custom-call(f32[512,128]{1,0:T(8,128)} %bitcast.5, f32[512,128]{1,0:T(8,128)} %bitcast.7, bf16[2,16,32,128]{3,2,1,0:T(8,128)(2,1)S(1)} %get-tuple-element.8.pieces_ref, bf16[8,288,128]{2,1,0:T(8,128)(2,1)S(1)} %get-tuple-element.9.grad_ref), custom_call_target="tpu_custom_call" | custom-call | tf_op jit(solution)/shard_map/pallas_call | solution.py:792

commit v7 on v6

--- a/solution.py
+++ b/solution.py
@@ -134,7 +134,21 @@
     def pack(src, n):
         def one(h, carry):
             x = src[pl.ds(h, 64, stride=8), :]
-            snd[n, h] = x.astype(BF)
+            turned_by = jnp.where(top, 64, 0)
+            middle = jnp.where(
+                lane32 < 64,
+                pltpu.roll(x[:32], turned_by, 1),
+                pltpu.roll(x[32:], 64 - turned_by, 1),
+            )
+            flank = jnp.zeros((16, 128), F32)
+            for g in range(4):
+                part = pltpu.roll(
+                    x[16 * g : 16 * g + 16],
+                    jnp.where(top, (32 * g + 96) % 128, (32 * g + 64) % 128),
+                    1,
+                )
+                flank = jnp.where(lane16 // 32 == g, part, flank)
+            snd[n, h] = jnp.concatenate([middle, flank], axis=0).astype(BF)
             for side in range(2):
                 edge = jnp.zeros((16, 128), F32)
                 for g in range(4):
@@ -264,6 +278,9 @@
     def _():
         gain_rcv[layer] = gain_snd[...]
 
+    def spread(packed):
+        return jnp.concatenate([pltpu.roll(packed, 32, 1), pltpu.roll(packed, 96, 1)], axis=0)
+
     def assemble(src, n, dst):
         shift = jnp.where(top, 32, 96)
 
@@ -279,13 +296,24 @@
 
         start = jnp.where(top, 0, 96)
         outer = (lane >= start) & (lane < start + 32)
+        middle = (lane >= 32) & (lane < 96)
 
         def one(h, carry):
             x = src[pl.ds(h, 64, stride=8), :]
             dst[8 * row + h] = jnp.where(outer, halo(row, h), pltpu.roll(x, shift, 1)) * inside
             y = rcv[n, h].astype(F32)
+            flank = jnp.concatenate(
+                [
+                    pltpu.roll(
+                        y[32:48], jnp.where(top, (96 - 32 * g) % 128, (128 - 32 * g) % 128), 1
+                    )
+                    for g in range(4)
+                ],
+                axis=0,
+            )
             dst[8 * (1 - row) + h] = (
-                jnp.where(outer, halo(1 - row, h), pltpu.roll(y, shift, 1)) * inside
+                jnp.where(outer, halo(1 - row, h), jnp.where(middle, spread(y[:32]), flank))
+                * inside
             )
             return carry
 
@@ -339,10 +367,10 @@
         shift = jnp.where(top, 32, 96)
         for u in range(8):
             for rho, guess in (
-                (row, guess_own[pl.ds(u, 64, stride=8), :]),
-                (1 - row, rcv[n, u].astype(F32)),
+                (row, pltpu.roll(guess_own[pl.ds(u, 64, stride=8), :], shift, 1)),
+                (1 - row, spread(rcv[n, u, 0:32, :].astype(F32))),
             ):
-                r = field[8 * rho + u] - gain * pltpu.roll(guess, shift, 1)
+                r = field[8 * rho + u] - gain * guess
                 p1_snd[n, 8 * rho + u] = jnp.where(
                     lane32 < 64, pltpu.roll(r[:32], 96, 1), pltpu.roll(r[32:], 32, 1)
                 ).astype(BF)
@@ -682,8 +710,8 @@
         in_specs=[pl.BlockSpec(memory_space=pltpu.HBM)] * 5,
         out_specs=[pl.BlockSpec(memory_space=vm)] * 2,
         scratch_shapes=[
-            vm((2, 8, 64, 128), BF),
-            vm((2, 8, 64, 128), BF),
+            vm((2, 8, 48, 128), BF),
+            vm((2, 8, 48, 128), BF),
             vm((2, 2, 8, 16, 128), BF),
             vm((2, 2, 8, 16, 128), BF),
             vm((128, 128), F32),

time: 43.7 us -> 43 us (0.984)
  Pallas kernels: 42.9 us -> 42.2 us
    pallas_call x1, Pallas kernels: 41.1 us -> 40.3 us  [fused(): pl.pallas_call(fused_kernel, out_shape=(jax.ShapeDtypeStruct((2, 16, 32,...]
where the time goes in v7:
time: 43 us; the launch traced here: 42.8 us
  Pallas kernels  42.2 us (98%)
  between operations  0.64 us (1%)
    pallas_call x1, Pallas kernels, fused(): pl.pallas_call(fused_kernel, out_shape=(jax.ShapeDtypeStruct((2, 16, 32,...  40.3 us
    pallas_call x1, Pallas kernels, unpack(): pl.pallas_call(unpack_kernel, out_shape=(jax.ShapeDtypeStruct((512, 128),...  1.89 us

profile of v7, /device:TPU:1, one launch (start us, length us, event | category | flops | bytes accessed | tf_op | source)
XLA Modules:
  0.0 42.8 jit_solution(18072661477999030669)
XLA Ops:
  0.6 40.3 %shard_map.76 = (bf16[2,16,32,128]{3,2,1,0:T(8,128)(2,1)S(1)}, bf16[8,288,128]{2,1,0:T(8,128)(2,1)S(1)}) custom-call(f32[512,128]{1,0:T(8,128)} %bitcast.4, f32[512,128]{1,0:T(8,128)} %bitcast.6, bf16[8,9,64,64]{3,2,1,0:T(8,128)(2,1)} %w_hbm.1, f32[8,64]{1,0:T(8,128)} %b_hbm.1, f32[1,64]{1,0:T(1,128)} %gain_hbm.1), custom_call_target="tpu_custom_call" | custom-call | tf_op jit(solution)/shard_map/pallas_call | solution.py:704
  40.9 1.9 %shard_map.77 = (f32[512,128]{1,0:T(8,128)}, f32[512,128]{1,0:T(8,128)}, f32[8,9,64,64]{3,2,1,0:T(8,128)}) custom-call(f32[512,128]{1,0:T(8,128)} %bitcast.5, f32[512,128]{1,0:T(8,128)} %bitcast.7, bf16[2,16,32,128]{3,2,1,0:T(8,128)(2,1)S(1)} %get-tuple-element.8.pieces_ref, bf16[8,288,128]{2,1,0:T(8,128)(2,1)S(1)} %get-tuple-element.9.grad_ref), custom_call_target="tpu_custom_call" | custom-call | tf_op jit(solution)/shard_map/pallas_call | solution.py:820

commit v8 on v7

--- a/solution.py
+++ b/solution.py
@@ -595,9 +595,9 @@
             ),
         )
 
-        @pl.when(step >= SPLIT + 1)
-        def _():
-            to_owner(l + 3)
+        @pl.when(step >= SPLIT)
+        def _():
+            to_owner(l + 2)
 
         @pl.when(step == 5)
         def _():
@@ -606,7 +606,7 @@
         return carry
 
     lax.fori_loop(SPLIT, blocks, weight_grads, 0)
-    for l in (2, 1, 0):
+    for l in (1, 0):
         to_owner(l)
     solve(1)
     own_block(1)
@@ -627,8 +627,6 @@
 
         gd_copy(l).start()
         return carry
-
-    lax.fori_loop(0, blocks, forward_half, 0)
 
     for n in range(2):
         for copy in exchange(n):
@@ -653,6 +651,18 @@
 
     all_but_own(16, sent)
 
+    def drain_parts(l, carry):
+        ga_copy(l).wait_send()
+
+        @pl.when(lax.rem(l, 4) != chip)
+        def _():
+            gb_copy(l).wait_send()
+
+        return carry
+
+    lax.fori_loop(0, blocks, drain_parts, 0)
+    lax.fori_loop(0, blocks, forward_half, 0)
+
     def p2_bytes(n, count):
         return remote(
             p2_snd.at[n, pl.ds(0, count)],
@@ -675,12 +685,6 @@
             p2_bytes(n, 15).wait_recv()
 
     def drain_grads(l, carry):
-        ga_copy(l).wait_send()
-
-        @pl.when(lax.rem(l, 4) != chip)
-        def _():
-            gb_copy(l).wait_send()
-
         gd_copy(l).wait_send()
         remote(
             grad_out.at[l, other_half],

time: 43 us -> 42.9 us (level)
  no operation moved by 1% of the time
where the time goes in v8:
time: 42.9 us; the launch traced here: 42.7 us
  Pallas kernels  42.1 us (98%)
  between operations  0.64 us (1%)
    pallas_call x1, Pallas kernels, fused(): pl.pallas_call(fused_kernel, out_shape=(jax.ShapeDtypeStruct((2, 16, 32,...  40.2 us
    pallas_call x1, Pallas kernels, unpack(): pl.pallas_call(unpack_kernel, out_shape=(jax.ShapeDtypeStruct((512, 128),...  1.89 us

profile of v8, /device:TPU:1, one launch (start us, length us, event | category | flops | bytes accessed | tf_op | source)
XLA Modules:
  0.0 42.7 jit_solution(17136454857085481214)
XLA Ops:
  0.6 40.2 %shard_map.76 = (bf16[2,16,32,128]{3,2,1,0:T(8,128)(2,1)S(1)}, bf16[8,288,128]{2,1,0:T(8,128)(2,1)S(1)}) custom-call(f32[512,128]{1,0:T(8,128)} %bitcast.4, f32[512,128]{1,0:T(8,128)} %bitcast.6, bf16[8,9,64,64]{3,2,1,0:T(8,128)(2,1)} %w_hbm.1, f32[8,64]{1,0:T(8,128)} %b_hbm.1, f32[1,64]{1,0:T(1,128)} %gain_hbm.1), custom_call_target="tpu_custom_call" | custom-call | tf_op jit(solution)/shard_map/pallas_call | solution.py:708
  40.8 1.9 %shard_map.77 = (f32[512,128]{1,0:T(8,128)}, f32[512,128]{1,0:T(8,128)}, f32[8,9,64,64]{3,2,1,0:T(8,128)}) custom-call(f32[512,128]{1,0:T(8,128)} %bitcast.5, f32[512,128]{1,0:T(8,128)} %bitcast.7, bf16[2,16,32,128]{3,2,1,0:T(8,128)(2,1)S(1)} %get-tuple-element.8.pieces_ref, bf16[8,288,128]{2,1,0:T(8,128)(2,1)S(1)} %get-tuple-element.9.grad_ref), custom_call_target="tpu_custom_call" | custom-call | tf_op jit(solution)/shard_map/pallas_call | solution.py:824

commit v9 on v8

--- a/solution.py
+++ b/solution.py
@@ -160,7 +160,8 @@
                 edge_snd[side, n, h] = edge.astype(BF)
             return carry
 
-        lax.fori_loop(0, 8, one, 0)
+        for h in range(8):
+            one(h, 0)
 
     def exchange(n):
         yield remote(snd.at[n], rcv.at[n], in_send.at[n, 0], in_recv.at[n, 0], {"row": 1 - row})
@@ -317,7 +318,8 @@
             )
             return carry
 
-        lax.fori_loop(0, 8, one, 0)
+        for h in range(8):
+            one(h, 0)
 
     arrived(0)
     assemble(c_ref, 0, phi_ref)

time: 42.9 us -> 42 us (0.979)
  Pallas kernels: 42.1 us -> 41.2 us
    pallas_call x1, Pallas kernels: 40.2 us -> 39.3 us  [fused(): pl.pallas_call(fused_kernel, out_shape=(jax.ShapeDtypeStruct((2, 16, 32,...]
where the time goes in v9:
time: 42 us; the launch traced here: 41.9 us
  Pallas kernels  41.2 us (98%)
  between operations  0.64 us (2%)
    pallas_call x1, Pallas kernels, fused(): pl.pallas_call(fused_kernel, out_shape=(jax.ShapeDtypeStruct((2, 16, 32,...  39.3 us
    pallas_call x1, Pallas kernels, unpack(): pl.pallas_call(unpack_kernel, out_shape=(jax.ShapeDtypeStruct((512, 128),...  1.89 us

profile of v9, /device:TPU:1, one launch (start us, length us, event | category | flops | bytes accessed | tf_op | source)
XLA Modules:
  0.0 41.9 jit_solution(1587053806955370784)
XLA Ops:
  0.6 39.3 %shard_map.76 = (bf16[2,16,32,128]{3,2,1,0:T(8,128)(2,1)S(1)}, bf16[8,288,128]{2,1,0:T(8,128)(2,1)S(1)}) custom-call(f32[512,128]{1,0:T(8,128)} %bitcast.4, f32[512,128]{1,0:T(8,128)} %bitcast.6, bf16[8,9,64,64]{3,2,1,0:T(8,128)(2,1)} %w_hbm.1, f32[8,64]{1,0:T(8,128)} %b_hbm.1, f32[1,64]{1,0:T(1,128)} %gain_hbm.1), custom_call_target="tpu_custom_call" | custom-call | tf_op jit(solution)/shard_map/pallas_call | solution.py:710
  40.0 1.9 %shard_map.77 = (f32[512,128]{1,0:T(8,128)}, f32[512,128]{1,0:T(8,128)}, f32[8,9,64,64]{3,2,1,0:T(8,128)}) custom-call(f32[512,128]{1,0:T(8,128)} %bitcast.5, f32[512,128]{1,0:T(8,128)} %bitcast.7, bf16[2,16,32,128]{3,2,1,0:T(8,128)(2,1)S(1)} %get-tuple-element.8.pieces_ref, bf16[8,288,128]{2,1,0:T(8,128)(2,1)S(1)} %get-tuple-element.9.grad_ref), custom_call_target="tpu_custom_call" | custom-call | tf_op jit(solution)/shard_map/pallas_call | solution.py:826

commit v10 on v9

--- a/solution.py
+++ b/solution.py
@@ -108,8 +108,7 @@
             )
         )
     ]
-    for load in loads:
-        load.start()
+    loads[0].start()
 
     barrier = pltpu.get_barrier_semaphore()
 
@@ -192,6 +191,8 @@
             ).wait_recv()
 
     loads[0].wait()
+    for load in loads[1:]:
+        load.start()
     pack(c_ref, 0)
     pl.semaphore_wait(barrier, 2 * layers - 1 + 2 * (cols - 1))
     for copy in exchange(0):

time: 42 us -> 42 us (level)
  no operation moved by 1% of the time
where the time goes in v10:
time: 42 us; the launch traced here: 41.9 us
  Pallas kernels  41.2 us (98%)
  between operations  0.64 us (2%)
    pallas_call x1, Pallas kernels, fused(): pl.pallas_call(fused_kernel, out_shape=(jax.ShapeDtypeStruct((2, 16, 32,...  39.3 us
    pallas_call x1, Pallas kernels, unpack(): pl.pallas_call(unpack_kernel, out_shape=(jax.ShapeDtypeStruct((512, 128),...  1.89 us

profile of v10, /device:TPU:1, one launch (start us, length us, event | category | flops | bytes accessed | tf_op | source)
XLA Modules:
  0.0 41.9 jit_solution(10465754854827245003)
XLA Ops:
  0.6 39.3 %shard_map.76 = (bf16[2,16,32,128]{3,2,1,0:T(8,128)(2,1)S(1)}, bf16[8,288,128]{2,1,0:T(8,128)(2,1)S(1)}) custom-call(f32[512,128]{1,0:T(8,128)} %bitcast.4, f32[512,128]{1,0:T(8,128)} %bitcast.6, bf16[8,9,64,64]{3,2,1,0:T(8,128)(2,1)} %w_hbm.1, f32[8,64]{1,0:T(8,128)} %b_hbm.1, f32[1,64]{1,0:T(1,128)} %gain_hbm.1), custom_call_target="tpu_custom_call" | custom-call | tf_op jit(solution)/shard_map/pallas_call | solution.py:711
  40.0 1.9 %shard_map.77 = (f32[512,128]{1,0:T(8,128)}, f32[512,128]{1,0:T(8,128)}, f32[8,9,64,64]{3,2,1,0:T(8,128)}) custom-call(f32[512,128]{1,0:T(8,128)} %bitcast.5, f32[512,128]{1,0:T(8,128)} %bitcast.7, bf16[2,16,32,128]{3,2,1,0:T(8,128)(2,1)S(1)} %get-tuple-element.8.pieces_ref, bf16[8,288,128]{2,1,0:T(8,128)(2,1)S(1)} %get-tuple-element.9.grad_ref), custom_call_target="tpu_custom_call" | custom-call | tf_op jit(solution)/shard_map/pallas_call | solution.py:827
